TPU v7x, 512 devices: a whole 4x8x8 slice. The times are simulated.
512 devices in a mesh: dp: 2 (over z_hi), row: 16 (over y, core), col: 16 (over x, z_lo).
Axes of the slice: x: 4, y: 8, z: 8 (z_hi: 2, z_lo: 4; z = z_hi * 4 + z_lo), core: 2. Of those that a mesh axis runs over, the one named last changes fastest.
Arguments:
- tokens: bfloat16 [512, 8192], P(('dp', 'col'), 'row'), may hold values from -6 to 6
- cotangent: bfloat16 [512, 8192], P(('dp', 'col'), 'row'), may hold values from -6 to 6
- gate_blocks: bfloat16 [16, 16, 21, 128, 128], P('row', 'col'), may hold values from -0.09375 to 0.09375
- gate_index: int32 [16, 16, 21, 2], P('row', 'col'), may hold values from -1 to 6, as said below
- up_blocks: bfloat16 [16, 16, 21, 128, 128], P('row', 'col'), may hold values from -0.09375 to 0.09375
- up_index: int32 [16, 16, 21, 2], P('row', 'col'), may hold values from -1 to 6, as said below
- down_blocks: bfloat16 [16, 16, 21, 128, 128], P('row', 'col'), may hold values from -0.0625 to 0.0625
- down_index: int32 [16, 16, 21, 2], P('row', 'col'), may hold values from -1 to 6, as said below
Outputs:
- output: bfloat16 [512, 8192], P(('dp', 'col'), 'row')
- input_grad: bfloat16 [512, 8192], P(('dp', 'col'), 'row')
- gate_grad: bfloat16 [16, 16, 21, 128, 128], P('row', 'col')
- up_grad: bfloat16 [16, 16, 21, 128, 128], P('row', 'col')
- down_grad: bfloat16 [16, 16, 21, 128, 128], P('row', 'col')
Inputs may be any that keep to these rules, and one draw needn't show every extreme that they name: `gate_index`: in each tile the listed slots come first and name distinct positions, with a first entry below 4 and a second below 7; every slot after them holds -1 in both entries. A tile lists 7 to 21 blocks, and some tile lists exactly 21. `up_index`: as for gate_index, with a pattern of its own. `down_index`: as for gate_index with the entries' roles swapped: the first is below 7, the second below 4. A tile lists 7 to 21 blocks, and some tile lists exactly 21.
All inputs are finite; a program needn't handle non-finite values.
Results may differ from a plain program's by a relative error of at most 0.0059.
Values may be sent and summed in bfloat16 or wider, within the bound.
A program may use at most 64 MiB of HBM per device.

v0:
```python
import math

import jax
import jax.numpy as jnp
from jax import lax
from jax.sharding import PartitionSpec as P

FF = 14336
BLK = 128


def sent_together(arrays, axis, dim, along):
    both = jnp.concatenate(arrays, axis=along)
    out, at, gathered = (lax.all_gather(both, axis, axis=dim, tiled=True), 0, [])
    for a in arrays:
        gathered.append(lax.slice_in_dim(out, at, at + a.shape[along], axis=along))
        at += a.shape[along]
    return tuple(gathered)


def cut_along(shard, dim, size):
    dims = shard.shape
    tiles = shard.reshape(*dims[:dim], size, dims[dim] // size, *dims[dim + 1 :])
    return jnp.moveaxis(tiles, dim, 0)


def sum_at_owner(shard, axis, dim):
    tiles = cut_along(shard, dim, lax.axis_size(axis))
    arrived = lax.all_to_all(tiles, axis, split_axis=0, concat_axis=0, tiled=True)
    return arrived.sum(axis=0)


def in_order(tiles, dim):
    dims = list(tiles.shape[1:])
    dims[dim] *= tiles.shape[0]
    return jnp.moveaxis(tiles, 0, dim).reshape(dims)


def copy_for_each(shard, axis):
    copies = jnp.broadcast_to(shard, (lax.axis_size(axis), *shard.shape))
    return lax.all_to_all(copies, axis, split_axis=0, concat_axis=0, tiled=True)


def gathered_copies(shard, axis, dim):
    return in_order(copy_for_each(shard, axis), dim)


def taken_together(shard, axis):
    return copy_for_each(shard, axis).astype(jnp.float32).sum(axis=0)


def one_hots(index_list, row_count, col_count):
    row_hot = (index_list[:, 0:1] == jnp.arange(row_count, dtype=jnp.int32)[None, :]).astype(
        jnp.bfloat16
    )
    col_hot = (index_list[:, 1:2] == jnp.arange(col_count, dtype=jnp.int32)[None, :]).astype(
        jnp.bfloat16
    )
    return (row_hot, col_hot)


def dense_tools(blocks, index_list, row_count, col_count):
    blocks = blocks[0, 0]
    listing = index_list[0, 0]
    row_hot, col_hot = one_hots(listing, row_count, col_count)
    listed = listing[:, 0] >= 0
    row_ids = jnp.maximum(listing[:, 0], 0)
    col_ids = jnp.maximum(listing[:, 1], 0)
    width = blocks.shape[1]
    dense = jnp.einsum(
        "kr,kc,kab->racb", row_hot, col_hot, blocks, preferred_element_type=jnp.float32
    )
    dense = dense.astype(jnp.bfloat16).reshape(row_count * width, col_count * width)

    def apply_tile(panel):
        return jnp.dot(panel, dense, preferred_element_type=jnp.float32)

    def apply_back(panel):
        return lax.dot_general(
            panel, dense, (((1,), (1,)), ((), ())), preferred_element_type=jnp.float32
        )

    def block_grads(left, right):
        full = lax.dot_general(
            left, right, (((0,), (0,)), ((), ())), preferred_element_type=jnp.float32
        )
        shaped = full.reshape(row_count, width, col_count, width).transpose(0, 2, 1, 3)
        picked = shaped[row_ids, col_ids]
        return jnp.where(listed[:, None, None], picked, jnp.float32(0.0))

    return (apply_tile, apply_back, block_grads)


def on_device(
    tokens, cotangent, gate_blocks, gate_index, up_blocks, up_index, down_blocks, down_index
):
    feat_count = tokens.shape[1] // BLK
    unit_count = FF // BLK // lax.axis_size("col")
    unit_width = unit_count * BLK
    panel_x, panel_d = sent_together((tokens, cotangent), "col", 0, 1)
    group_rows = panel_x.shape[0]
    scale = 1.0 / math.sqrt(group_rows * lax.axis_size("dp"))
    gate_fwd, gate_back, gate_grads = dense_tools(gate_blocks, gate_index, feat_count, unit_count)
    up_fwd, up_back, up_grads = dense_tools(up_blocks, up_index, feat_count, unit_count)
    down_fwd, down_back, down_grads = dense_tools(down_blocks, down_index, unit_count, feat_count)
    both = sum_at_owner(jnp.concatenate([gate_fwd(panel_x), up_fwd(panel_x)], axis=1), "row", 0)
    gate_part = both[:, :unit_width]
    up_part = both[:, unit_width:]
    hidden_part = (gate_part * jax.nn.sigmoid(gate_part) * up_part).astype(jnp.bfloat16)
    hidden_all = gathered_copies(hidden_part, "row", 0)
    output = sum_at_owner(down_fwd(hidden_all), "col", 0).astype(jnp.bfloat16)
    grad_hidden = sum_at_owner(down_back(panel_d), "row", 0)
    sigma = jax.nn.sigmoid(gate_part)
    grad_gate = (grad_hidden * up_part * sigma * (1.0 + gate_part * (1.0 - sigma))).astype(
        jnp.bfloat16
    )
    grad_up = (grad_hidden * gate_part * sigma).astype(jnp.bfloat16)
    gate_grad_all, up_grad_all = sent_together((grad_gate, grad_up), "row", 0, 1)
    input_grad = sum_at_owner(gate_back(gate_grad_all) + up_back(up_grad_all), "col", 0).astype(
        jnp.bfloat16
    )
    gate_local = gate_grads(panel_x, gate_grad_all) * scale
    up_local = up_grads(panel_x, up_grad_all) * scale
    down_local = down_grads(hidden_all, panel_d) * scale
    gate_sum, up_sum, down_sum = (
        taken_together(gate_local.astype(jnp.bfloat16), "dp").astype(jnp.float32),
        taken_together(up_local.astype(jnp.bfloat16), "dp").astype(jnp.float32),
        taken_together(down_local.astype(jnp.bfloat16), "dp").astype(jnp.float32),
    )
    gate_grad = gate_sum.astype(jnp.bfloat16).reshape(gate_blocks.shape)
    up_grad = up_sum.astype(jnp.bfloat16).reshape(up_blocks.shape)
    down_grad = down_sum.astype(jnp.bfloat16).reshape(down_blocks.shape)
    return (output, input_grad, gate_grad, up_grad, down_grad)


def solution(mesh):
    return jax.shard_map(
        on_device,
        mesh=mesh,
        in_specs=(
            P(("dp", "col"), "row"),
            P(("dp", "col"), "row"),
            P("row", "col", None, None, None),
            P("row", "col", None, None),
            P("row", "col", None, None, None),
            P("row", "col", None, None),
            P("row", "col", None, None, None),
            P("row", "col", None, None),
        ),
        out_specs=(
            P(("dp", "col"), "row"),
            P(("dp", "col"), "row"),
            P("row", "col", None, None, None),
            P("row", "col", None, None, None),
            P("row", "col", None, None, None),
        ),
        check_vma=False,
    )
```

profile of v0, /device:TPU:8, one launch (start us, length us, event | category | flops | bytes accessed | tf_op | source)
XLA Modules:
  0.0 334.7 jit_solution(16868386810082536184)
XLA Ops:
  0.6 0.7 pad_maximum_fusion.2
  1.4 49.8 %all_gather.6 = bf16[256,1024]{1,0:T(8,128)(2,1)S(1)} all-gather(bf16[16,1024]{1,0:T(8,128)(2,1)S(1)} %pad_maximum_fusion.2), channel_id=1, replica_groups=mesh['dp'=2,'row'=16,'col'=16] {'col'}, dimensions={0}, use_global_device_ids=true | all-gather | bytes 557056 | tf_op jit(solution)/shard_map/all_gather | solution.py:14
  51.2 0.8 or_bitcast_fusion
  52.0 1.8 fusion
  53.8 0.8 copy.35
  54.9 0.7 slice_bitcast_fusion.6
  55.6 1.4 fusion.47
  57.1 7.7 %all-to-all-start.3 = ((f32[16,16,896]{2,1,0:T(8,128)}), f32[16,16,896]{2,1,0:T(8,128)S(1)}, u32[]{:S(2)}, u32[]{:S(2)}) async-start(f32[16,16,896]{2,1,0:T(8,128)} %fusion.47), calls=%async_computation.3 | async-start | bytes 1835008 | tf_op jit(solution)/shard_map/all_to_all | solution.py:29
  64.9 1.9 convolution_convert_fusion.1
  68.9 1.3 pad_maximum_fusion
  70.2 16.4 %all-to-all-done.3 = f32[16,16,896]{2,1,0:T(8,128)S(1)} async-done(((f32[16,16,896]{2,1,0:T(8,128)}), f32[16,16,896]{2,1,0:T(8,128)S(1)}, u32[]{:S(2)}, u32[]{:S(2)}) %all-to-all-start.3) | async-done | bytes 917536 | tf_op jit(solution)/shard_map/all_to_all | solution.py:29
  86.6 6.8 %all-to-all-start = ((f32[16,16,1792]{2,1,0:T(8,128)}), f32[16,16,1792]{2,1,0:T(8,128)}, u32[]{:S(2)}, u32[]{:S(2)}) async-start(f32[16,16,1792]{2,1,0:T(8,128)} %bitcast.107), calls=%async_computation | async-start | bytes 3670016 | tf_op jit(solution)/shard_map/all_to_all | solution.py:29
  93.4 41.5 %all-to-all-done = f32[16,16,1792]{2,1,0:T(8,128)} async-done(((f32[16,16,1792]{2,1,0:T(8,128)}), f32[16,16,1792]{2,1,0:T(8,128)}, u32[]{:S(2)}, u32[]{:S(2)}) %all-to-all-start) | async-done | bytes 1835040 | tf_op jit(solution)/shard_map/all_to_all | solution.py:29
  135.0 1.6 reduce_sum.72
  136.6 0.8 broadcast_in_dim.51
  137.4 6.8 %all-to-all-start.1 = ((bf16[16,16,896]{2,1,0:T(8,128)(2,1)}), bf16[16,16,896]{2,1,0:T(8,128)(2,1)}, u32[]{:S(2)}, u32[]{:S(2)}) async-start(bf16[16,16,896]{2,1,0:T(8,128)(2,1)} %broadcast_in_dim.51), calls=%async_computation.1 | async-start | bytes 917504 | tf_op jit(solution)/shard_map/all_to_all | solution.py:41
  144.2 25.9 %all_gather.7 = bf16[256,1792]{1,0:T(8,128)(2,1)S(1)} all-gather(bf16[16,1792]{1,0:T(8,128)(2,1)S(1)} %pad_maximum_fusion.1), channel_id=1, replica_groups=mesh['dp'=2,'row'=16,'col'=16] {'row'}, dimensions={0}, use_global_device_ids=true | all-gather | bytes 974848 | tf_op jit(solution)/shard_map/all_gather | solution.py:14
  170.1 2.0 fusion.6
  172.1 1.3 convolution_add_fusion
  173.4 4.2 %all-to-all-start.4 = ((f32[16,16,512]{2,1,0:T(8,128)}), f32[16,16,512]{2,1,0:T(8,128)}, u32[]{:S(2)}, u32[]{:S(2)}) async-start(f32[16,16,512]{2,1,0:T(8,128)} %bitcast.112), calls=%async_computation.4 | async-start | bytes 1048576 | tf_op jit(solution)/shard_map/all_to_all | solution.py:29
  177.7 1.7 fusion.21
  179.4 1.9 reshape.71
  181.3 2.1 copy.37
  183.4 2.1 gather_fusion
  185.8 9.2 %all-to-all-done.4 = f32[16,16,512]{2,1,0:T(8,128)} async-done(((f32[16,16,512]{2,1,0:T(8,128)}), f32[16,16,512]{2,1,0:T(8,128)}, u32[]{:S(2)}, u32[]{:S(2)}) %all-to-all-start.4) | async-done | bytes 524320 | tf_op jit(solution)/shard_map/all_to_all | solution.py:29
  195.0 1.4 broadcast_in_dim.54
  196.4 7.5 %all-to-all-start.5 = ((bf16[2,21,128,128]{3,2,1,0:T(8,128)(2,1)}), bf16[2,21,128,128]{3,2,1,0:T(8,128)(2,1)}, u32[]{:S(2)}, u32[]{:S(2)}) async-start(bf16[2,21,128,128]{3,2,1,0:T(8,128)(2,1)} %broadcast_in_dim.54), calls=%async_computation.5 | async-start | bytes 2752512 | tf_op jit(solution)/shard_map/all_to_all | solution.py:41
  203.9 1.5 fusion.18
  205.4 1.9 reshape.73
  207.2 2.1 copy.39
  209.3 1.9 gather_fusion.1
  211.2 1.6 multiply_convert_fusion.1
  212.8 24.5 %all-to-all-done.5 = bf16[2,21,128,128]{3,2,1,0:T(8,128)(2,1)} async-done(((bf16[2,21,128,128]{3,2,1,0:T(8,128)(2,1)}), bf16[2,21,128,128]{3,2,1,0:T(8,128)(2,1)}, u32[]{:S(2)}, u32[]{:S(2)}) %all-to-all-start.5) | async-done | bytes 1376288 | tf_op jit(solution)/shard_map/all_to_all | solution.py:41
  237.3 1.4 broadcast_in_dim.56
  238.7 3.6 %all-to-all-start.6 = ((bf16[2,21,128,128]{3,2,1,0:T(8,128)(2,1)}), bf16[2,21,128,128]{3,2,1,0:T(8,128)(2,1)S(1)}, u32[]{:S(2)}, u32[]{:S(2)}) async-start(bf16[2,21,128,128]{3,2,1,0:T(8,128)(2,1)} %broadcast_in_dim.56), calls=%async_computation.6 | async-start | bytes 2752512 | tf_op jit(solution)/shard_map/all_to_all | solution.py:41
  242.4 2.3 fusion.46
  244.7 28.6 %all-to-all-done.6 = bf16[2,21,128,128]{3,2,1,0:T(8,128)(2,1)S(1)} async-done(((bf16[2,21,128,128]{3,2,1,0:T(8,128)(2,1)}), bf16[2,21,128,128]{3,2,1,0:T(8,128)(2,1)S(1)}, u32[]{:S(2)}, u32[]{:S(2)}) %all-to-all-start.6) | async-done | bytes 1376288 | tf_op jit(solution)/shard_map/all_to_all | solution.py:41
  273.2 5.3 %all-to-all-start.2 = ((f32[16,16,512]{2,1,0:T(8,128)}), f32[16,16,512]{2,1,0:T(8,128)}, u32[]{:S(2)}, u32[]{:S(2)}) async-start(f32[16,16,512]{2,1,0:T(8,128)} %fusion.46), calls=%async_computation.2 | async-start | bytes 1048576 | tf_op jit(solution)/shard_map/all_to_all | solution.py:29
  278.7 1.2 copy.40
  281.3 13.8 %all-to-all-done.2 = f32[16,16,512]{2,1,0:T(8,128)} async-done(((f32[16,16,512]{2,1,0:T(8,128)}), f32[16,16,512]{2,1,0:T(8,128)}, u32[]{:S(2)}, u32[]{:S(2)}) %all-to-all-start.2) | async-done | bytes 524320 | tf_op jit(solution)/shard_map/all_to_all | solution.py:29
  295.1 1.4 broadcast_in_dim.58
  296.5 3.9 %all-to-all-start.7 = ((bf16[2,21,128,128]{3,2,1,0:T(8,128)(2,1)}), bf16[2,21,128,128]{3,2,1,0:T(8,128)(2,1)S(1)}, u32[]{:S(2)}, u32[]{:S(2)}) async-start(bf16[2,21,128,128]{3,2,1,0:T(8,128)(2,1)} %broadcast_in_dim.58), calls=%async_computation.7 | async-start | bytes 2752512 | tf_op jit(solution)/shard_map/all_to_all | solution.py:41
  300.4 1.8 reduce_sum.75
  302.2 2.6 reduce_sum.76
  304.8 1.3 reduce_sum.77
  306.1 1.7 reduce_sum.73
  307.8 25.6 %all-to-all-done.7 = bf16[2,21,128,128]{3,2,1,0:T(8,128)(2,1)S(1)} async-done(((bf16[2,21,128,128]{3,2,1,0:T(8,128)(2,1)}), bf16[2,21,128,128]{3,2,1,0:T(8,128)(2,1)S(1)}, u32[]{:S(2)}, u32[]{:S(2)}) %all-to-all-start.7) | async-done | bytes 1376288 | tf_op jit(solution)/shard_map/all_to_all | solution.py:41
  333.4 1.3 reduce_sum.78
  (42 shorter events, 4.4 us)
Async XLA Ops:
  57.1 7.7 %copy-start.7 = (s32[1,1,21,2]{2,3,1,0:T(2,128)S(1)}, s32[1,1,21,2]{2,3,1,0:T(2,128)}, u32[]{:S(2)}) copy-start(s32[1,1,21,2]{2,3,1,0:T(2,128)} %param.13) | copy-start | bytes 508
  57.1 7.8 %copy-start.6 = (s32[1,1,21,2]{2,3,1,0:T(2,128)S(1)}, s32[1,1,21,2]{2,3,1,0:T(2,128)}, u32[]{:S(2)}) copy-start(s32[1,1,21,2]{2,3,1,0:T(2,128)} %param.11) | copy-start | bytes 508
  57.1 29.5 %all-to-all-start.3 = ((f32[16,16,896]{2,1,0:T(8,128)}), f32[16,16,896]{2,1,0:T(8,128)S(1)}, u32[]{:S(2)}, u32[]{:S(2)}) async-start(f32[16,16,896]{2,1,0:T(8,128)} %fusion.47), calls=%async_computation.3 | async-start | bytes 1835008 | tf_op jit(solution)/shard_map/all_to_all | solution.py:29
  64.8 2.0 copy-start.5
  67.5 1.0 copy-start.3
  86.6 48.4 %all-to-all-start = ((f32[16,16,1792]{2,1,0:T(8,128)}), f32[16,16,1792]{2,1,0:T(8,128)}, u32[]{:S(2)}, u32[]{:S(2)}) async-start(f32[16,16,1792]{2,1,0:T(8,128)} %bitcast.107), calls=%async_computation | async-start | bytes 3670016 | tf_op jit(solution)/shard_map/all_to_all | solution.py:29
  137.4 36.0 %all-to-all-start.1 = ((bf16[16,16,896]{2,1,0:T(8,128)(2,1)}), bf16[16,16,896]{2,1,0:T(8,128)(2,1)}, u32[]{:S(2)}, u32[]{:S(2)}) async-start(bf16[16,16,896]{2,1,0:T(8,128)(2,1)} %broadcast_in_dim.51), calls=%async_computation.1 | async-start | bytes 917504 | tf_op jit(solution)/shard_map/all_to_all | solution.py:41
  170.1 7.6 %copy-start = (bf16[256,1792]{1,0:T(8,128)(2,1)}, bf16[256,1792]{1,0:T(8,128)(2,1)S(1)}, u32[]{:S(2)}) copy-start(bf16[256,1792]{1,0:T(8,128)(2,1)S(1)} %all_gather.7) | copy-start | bytes 2752516
  173.4 21.6 %all-to-all-start.4 = ((f32[16,16,512]{2,1,0:T(8,128)}), f32[16,16,512]{2,1,0:T(8,128)}, u32[]{:S(2)}, u32[]{:S(2)}) async-start(f32[16,16,512]{2,1,0:T(8,128)} %bitcast.112), calls=%async_computation.4 | async-start | bytes 1048576 | tf_op jit(solution)/shard_map/all_to_all | solution.py:29
  196.4 40.9 %all-to-all-start.5 = ((bf16[2,21,128,128]{3,2,1,0:T(8,128)(2,1)}), bf16[2,21,128,128]{3,2,1,0:T(8,128)(2,1)}, u32[]{:S(2)}, u32[]{:S(2)}) async-start(bf16[2,21,128,128]{3,2,1,0:T(8,128)(2,1)} %broadcast_in_dim.54), calls=%async_computation.5 | async-start | bytes 2752512 | tf_op jit(solution)/shard_map/all_to_all | solution.py:41
  238.7 34.5 %all-to-all-start.6 = ((bf16[2,21,128,128]{3,2,1,0:T(8,128)(2,1)}), bf16[2,21,128,128]{3,2,1,0:T(8,128)(2,1)S(1)}, u32[]{:S(2)}, u32[]{:S(2)}) async-start(bf16[2,21,128,128]{3,2,1,0:T(8,128)(2,1)} %broadcast_in_dim.56), calls=%async_computation.6 | async-start | bytes 2752512 | tf_op jit(solution)/shard_map/all_to_all | solution.py:41
  242.4 36.2 %copy-start.4 = (bf16[512,256]{0,1:T(8,128)(2,1)S(1)}, bf16[512,256]{0,1:T(8,128)(2,1)}, u32[]{:S(2)}) copy-start(bf16[512,256]{0,1:T(8,128)(2,1)} %get-tuple-element.5) | copy-start | bytes 786436
  242.4 36.3 %copy-start.8 = (s32[1,1,21,2]{2,3,1,0:T(2,128)S(1)}, s32[1,1,21,2]{2,3,1,0:T(2,128)}, u32[]{:S(2)}) copy-start(s32[1,1,21,2]{2,3,1,0:T(2,128)} %param.15) | copy-start | bytes 508
  273.2 6.7 %copy-start.1 = (bf16[2,21,128,128]{3,2,1,0:T(8,128)(2,1)}, bf16[2,21,128,128]{3,2,1,0:T(8,128)(2,1)S(1)}, u32[]{:S(2)}) copy-start(bf16[2,21,128,128]{3,2,1,0:T(8,128)(2,1)S(1)} %all-to-all-done.6) | copy-start | bytes 4128772
  273.2 21.8 %all-to-all-start.2 = ((f32[16,16,512]{2,1,0:T(8,128)}), f32[16,16,512]{2,1,0:T(8,128)}, u32[]{:S(2)}, u32[]{:S(2)}) async-start(f32[16,16,512]{2,1,0:T(8,128)} %fusion.46), calls=%async_computation.2 | async-start | bytes 1048576 | tf_op jit(solution)/shard_map/all_to_all | solution.py:29
  296.5 36.9 %all-to-all-start.7 = ((bf16[2,21,128,128]{3,2,1,0:T(8,128)(2,1)}), bf16[2,21,128,128]{3,2,1,0:T(8,128)(2,1)S(1)}, u32[]{:S(2)}, u32[]{:S(2)}) async-start(bf16[2,21,128,128]{3,2,1,0:T(8,128)(2,1)} %broadcast_in_dim.58), calls=%async_computation.7 | async-start | bytes 2752512 | tf_op jit(solution)/shard_map/all_to_all | solution.py:41
  300.4 4.4 %copy-start.2 = (bf16[2,21,128,128]{3,2,1,0:T(8,128)(2,1)S(1)}, bf16[2,21,128,128]{3,2,1,0:T(8,128)(2,1)}, u32[]{:S(2)}) copy-start(bf16[2,21,128,128]{3,2,1,0:T(8,128)(2,1)} %copy-done.1) | copy-start | bytes 4128772
where the time goes:
time: 336 us; the launch traced here: 335 us
  waiting for transfers between devices  160 us (48%)
  blocking collectives  75.7 us (23%)
  starting transfers between devices  45.8 us (14%)
  local copies, waits for them, and re-layouts  21.5 us (6%)
  matrix products  15.9 us (5%)
  other arithmetic  15.4 us (5%)
    all_to_all x4, waiting for transfers between devices, sum_at_owner(): lax.all_to_all(tiles, axis, split_axis=0, concat_axis=0, tiled=True)  80.9 us
    all_to_all x4, waiting for transfers between devices, copy_for_each(): return lax.all_to_all(copies, axis, split_axis=0, concat_axis=0, tiled=True)  78.6 us
    all_gather x2, blocking collectives, sent_together(): lax.all_gather(both, axis, axis=dim, tiled=True)  75.7 us
    all_to_all x4, starting transfers between devices, sum_at_owner(): lax.all_to_all(tiles, axis, split_axis=0, concat_axis=0, tiled=True)  24 us
    all_to_all x4, starting transfers between devices, copy_for_each(): return lax.all_to_all(copies, axis, split_axis=0, concat_axis=0, tiled=True)  21.8 us
    reshape x4, local copies, waits for them, and re-layouts, block_grads(): full.reshape(row_count, width, col_count, width).transpose(0, 2, 1, 3)  7.84 us
  transfers between devices with their start and end apart: 8, of which 7 were waited for; matrix products, arithmetic and copies ran while one was open for 11% of the time, Pallas kernels for 0%

commit v1 on v0

v1 whole, which is shorter than its diff:
```python
import functools
import math

import jax
import jax.numpy as jnp
from jax import lax
from jax.experimental import pallas as pl
from jax.experimental.pallas import tpu as pltpu
from jax.sharding import PartitionSpec as P

BLK = 128
XS = 4
MESH = pl.DeviceIdType.MESH
BF = jnp.bfloat16
F32 = jnp.float32


def split_tiles(tiles, parts, whole=False):
    cuts = [(tiles * i) // parts for i in range(parts + 1)]
    if whole:
        cuts = sorted({t * (tiles // 3) + c for t in range(3) for c in (0, (tiles // 3 + 1) // 2)} | {tiles})
        parts = len(cuts) - 1
    return [(cuts[i] * BLK, cuts[i + 1] * BLK, -1 if i % 2 == 0 else 1) for i in range(parts)]


class Dims:
    def __init__(self, mesh_shape, tok_rows, feat, cap, units):
        self.T = tok_rows
        self.F = feat
        self.CAP = cap
        self.DB = feat // BLK
        self.FB = units
        self.HU = units * BLK
        self.N = 3 * self.HU
        self.X = XS
        self.Z = mesh_shape["col"] // XS
        self.Y = mesh_shape["row"] // 2
        self.LONG = self.Y // 2
        self.SHORT = self.Y // 2 - 1
        self.NCOL = mesh_shape["col"]
        self.NROW = mesh_shape["row"]
        self.R = self.NCOL * self.T
        self.HALF = self.Y * self.T
        self.SL = self.DB * self.FB
        self.RS = split_tiles(3 * self.FB, 6, True)
        self.AG = split_tiles(3 * self.FB, 4)
        self.NSEM = 256


def main_kernel(
    d, gi, ui, di, tok, cot, gb, ub, db,
    o_out, ig_out, g_out, u_out, d_out,
    inv, wb0, wb1, wb2, wgu, wd, xr, xp, psend, precv, s1, rlong, slong, rshort, sshort, tot, hall,
    po, xsend, xrecv, zs, zsend, zrecv, fin, xt, ht, acc_gu, acc_d, dg, du, dd, pg, pu, pd,
    lsem, ssem, rsem,
):
    g = lax.axis_index("dp")
    row = lax.axis_index("row")
    col = lax.axis_index("col")
    y, k = lax.div(row, 2), lax.rem(row, 2)
    x, z = lax.div(col, d.Z), lax.rem(col, d.Z)
    T, F, HU, N, R = d.T, d.F, d.HU, d.N, d.R
    GU = 2 * HU
    ZT = d.Z * T
    wblk = (wb0, wb1, wb2)

    def ym(v):
        return lax.rem(y + v + 2 * d.Y, d.Y)

    def xm(v):
        return lax.rem(x + v + 2 * d.X, d.X)

    def zm(v):
        return lax.rem(z + v + 2 * d.Z, d.Z)

    def rows(start, size):
        return pl.ds(pl.multiple_of(start, size), size)

    def at_y(v):
        return {"row": ym(v) * 2 + k}

    def at_x(v):
        return {"col": xm(v) * d.Z + z}

    def at_z(v):
        return {"col": x * d.Z + zm(v)}

    def at_other_z(v):
        return {"dp": 1 - g, "col": x * d.Z + zm(v)}

    partner = {"row": y * 2 + 1 - k}

    sent = []
    ids = {}

    def number(name):
        if name not in ids:
            ids[name] = len(ids)
            assert len(ids) <= d.NSEM
        return ids[name]

    def send(name, src, dst, dev):
        i = number(name)
        c = pltpu.make_async_remote_copy(
            src_ref=src, dst_ref=dst, send_sem=ssem.at[i], recv_sem=rsem.at[i],
            device_id=dev, device_id_type=MESH,
        )
        c.start()
        sent.append(c)

    def recv(name, landing, dev):
        i = number(name)
        pltpu.make_async_remote_copy(
            src_ref=landing, dst_ref=landing, send_sem=ssem.at[i], recv_sem=rsem.at[i],
            device_id=dev, device_id_type=MESH,
        ).wait_recv()

    barrier = pltpu.get_barrier_semaphore()
    peers = [at_z(o) for o in range(1, d.Z)] + [at_other_z(o) for o in range(d.Z)]
    peers += [at_x(1), at_x(-1), at_y(1), at_y(-1), partner]
    for p in peers:
        pl.semaphore_signal(barrier, inc=1, device_id=p, device_id_type=MESH)

    own_rows = rows(col * T, T)
    loads = [
        pltpu.make_async_copy(tok, xr.at[0, own_rows], lsem.at[0]),
        pltpu.make_async_copy(cot, xr.at[1, own_rows], lsem.at[1]),
        pltpu.make_async_copy(gb, wb0.at[pl.ds(0, d.CAP)], lsem.at[2]),
        pltpu.make_async_copy(ub, wb1.at[pl.ds(0, d.CAP)], lsem.at[3]),
        pltpu.make_async_copy(db, wb2.at[pl.ds(0, d.CAP)], lsem.at[4]),
    ]
    for c in loads:
        c.start()

    pl.semaphore_wait(barrier, len(peers))

    def chunk(t, v, o):
        return xr.at[t, rows((xm(v) * d.Z + zm(-o)) * T, T)]

    def x_chunk(t, o, src):
        send(("xr", t, o), src, chunk(t, 0, o), at_x(1))
        send(("xl", t, o), src, chunk(t, 0, o), at_x(-1))

    def x_pass(t, o):
        m = 1 if t == 0 else -1
        side = "xr" if t == 0 else "xl"
        recv((side, t, o), chunk(t, -m, o), at_x(m))
        send(("xx", t, o), chunk(t, -m, o), chunk(t, -m, o), at_x(m))

    def x_end(t, o):
        m = 1 if t == 0 else -1
        side = "xl" if t == 0 else "xr"
        recv((side, t, o), chunk(t, m, o), at_x(-m))
        recv(("xx", t, o), chunk(t, 2, o), at_x(m))

    for t, src in ((0, tok), (1, cot)):
        for o in range(1, d.Z):
            send(("z0", t, o), src, xr.at[t, own_rows], at_z(o))
        x_chunk(t, 0, src)

    for t, (ref, per) in enumerate(((gi, d.FB), (ui, d.FB), (di, d.DB))):
        wblk[t][d.CAP] = jnp.zeros((BLK, BLK), BF)
        spots = [ref[0, s] * per + ref[1, s] for s in range(d.CAP)]

        def find(p, _, t=t, spots=spots):
            found = jnp.int32(d.CAP)
            for s in range(d.CAP):
                found = jnp.where(spots[s] == p, jnp.int32(s), found)
            inv[t * d.SL + p] = found
            return 0

        lax.fori_loop(0, d.SL, find, 0)

    def z_chunks(t):
        for o in range(1, d.Z):
            recv(("z0", t, o), chunk(t, 0, o), at_z(o))
            x_chunk(t, o, chunk(t, 0, o))

    def dense(t, per):
        loads[2 + t].wait()

        def put(p, _):
            i, j = lax.div(p, per), lax.rem(p, per)
            block = wblk[t][inv[t * d.SL + p]]
            if t < 2:
                wgu[rows(i * BLK, BLK), rows(j * BLK + t * HU, BLK)] = block
            else:
                wd[rows(i * BLK, BLK), rows(j * BLK, BLK)] = block
            return 0

        lax.fori_loop(0, d.SL, put, 0)

    z_chunks(0)
    z_chunks(1)

    other_rows = rows(R + col * T, T)
    for t, src in ((0, tok), (1, cot)):
        for o in range(d.Z):
            send(("z1", t, o), src, xr.at[t, other_rows], at_other_z(o))

    def z_other(t):
        for o in range(d.Z):
            recv(("z1", t, o), xr.at[t, rows(R + (x * d.Z + zm(-o)) * T, T)], at_z(o))

    def xblock(t, v):
        return xr.at[t, rows(R + xm(v) * ZT, ZT)]

    def b_send(t):
        send(("br", t), xblock(t, 0), xblock(t, 0), at_x(1))
        send(("bl", t), xblock(t, 0), xblock(t, 0), at_x(-1))

    def b_pass(t):
        m = 1 if t == 0 else -1
        recv(("br" if t == 0 else "bl", t), xblock(t, -m), at_x(m))
        send(("bb", t), xblock(t, -m), xblock(t, -m), at_x(m))

    def b_end(t):
        m = 1 if t == 0 else -1
        recv(("bl" if t == 0 else "br", t), xblock(t, m), at_x(-m))
        recv(("bb", t), xblock(t, 2), at_x(m))

    dense(0, d.FB)
    for o in range(d.Z):
        x_pass(0, o)
    dense(1, d.FB)
    for o in range(d.Z):
        x_pass(1, o)
    dense(2, d.DB)
    loads[0].wait()
    loads[1].wait()
    for t in (0, 1):
        for o in range(d.Z):
            x_end(t, o)

    def nt(a, b):
        return lax.dot_general(a, b, (((1,), (1,)), ((), ())), preferred_element_type=F32)

    def nn(a, b):
        return jnp.dot(a, b, preferred_element_type=F32)

    H = d.HALF
    for t in (0, 1):
        xp[t, 0:H] = xr[t, rows((1 - k) * H, H), :]
        xp[t, H : 2 * H] = xr[t, rows(k * H, H), :]
    for q, (a, b, _) in enumerate(d.RS):
        part = nn(xp[0], wgu[:, a:b]) if b <= GU else nt(xp[1], wd[a - GU : b - GU, :])
        psend[:, a:b] = part[0:H]
        send(("p", q), psend.at[:, a:b], precv.at[:, a:b], partner)
        s1[:, a:b] = part[H : 2 * H]

    def rs_long(s, q):
        a, b, m = d.RS[q]
        mine = s1[rows(ym(m * (d.LONG - s)) * T, T), a:b]
        if s > 0:
            recv(("rl", s - 1, q), rlong.at[s - 1, :, a:b], at_y(m))
            mine = mine + rlong[s - 1, :, a:b].astype(F32)
        slong[s, :, a:b] = mine.astype(BF)
        send(("rl", s, q), slong.at[s, :, a:b], rlong.at[s, :, a:b], at_y(m))

    def rs_short(s, q):
        a, b, m = d.RS[q]
        mine = s1[rows(ym(-m * (d.SHORT - s)) * T, T), a:b]
        if s > 0:
            recv(("rs", s - 1, q), rshort.at[s - 1, :, a:b], at_y(-m))
            mine = mine + rshort[s - 1, :, a:b].astype(F32)
        sshort[s, :, a:b] = mine.astype(BF)
        send(("rs", s, q), sshort.at[s, :, a:b], rshort.at[s, :, a:b], at_y(-m))

    for s in range(d.LONG):
        for q, (a, b, _) in enumerate(d.RS):
            if s == 0:
                recv(("p", q), precv.at[:, a:b], partner)
                s1[:, a:b] += precv[:, a:b]
            rs_long(s, q)
            if s < d.SHORT:
                rs_short(s, q)
        if s == 0:
            for t in (0, 1):
                z_other(t)
                b_send(t)
            xt[:, 0:R] = xr[0, 0:R, :].T
        if s == d.LONG - 1:
            b_pass(0)
            b_pass(1)
    for q, (a, b, m) in enumerate(d.RS):
        mine = s1[rows(y * T, T), a:b]
        if d.SHORT > 0:
            recv(("rs", d.SHORT - 1, q), rshort.at[d.SHORT - 1, :, a:b], at_y(-m))
            mine = mine + rshort[d.SHORT - 1, :, a:b].astype(F32)
        recv(("rl", d.LONG - 1, q), rlong.at[d.LONG - 1, :, a:b], at_y(m))
        tot[:, a:b] = mine + rlong[d.LONG - 1, :, a:b].astype(F32)

    gate, up, gh = tot[:, 0:HU], tot[:, HU:GU], tot[:, GU:N]
    sig = jax.nn.sigmoid(gate)
    mine_rows = rows((k * d.Y + y) * T, T)
    hall[mine_rows, 0:HU] = (gate * sig * up).astype(BF)
    hall[mine_rows, HU:GU] = (gh * up * sig * (1.0 + gate * (1.0 - sig))).astype(BF)
    hall[mine_rows, GU:N] = (gh * gate * sig).astype(BF)

    def hrows(gs, kk, yy):
        return rows(gs * R + (kk * d.Y + yy) * T, T)

    def ag_send(gs, s, q, long):
        a, b, m = d.AG[q]
        m = m if long else -m
        ref = hall.at[hrows(gs, k, ym(-m * s)), a:b]
        send(("al" if long else "as", gs, s, q), ref, ref, at_y(m))

    def ag_recv(gs, s, q, long):
        a, b, m = d.AG[q]
        m = m if long else -m
        ref = hall.at[hrows(gs, k, ym(-m * s)), a:b]
        recv(("al" if long else "as", gs, s - 1, q), ref, at_y(m))

    def to_partner(gs, v):
        ref = hall.at[hrows(gs, k, ym(v))]
        send(("ap", gs, v), ref, ref, partner)

    def ag_start(gs):
        for q in range(len(d.AG)):
            ag_send(gs, 0, q, True)
            if d.SHORT > 0:
                ag_send(gs, 0, q, False)
        to_partner(gs, 0)

    def ag_step(gs, s):
        for q in range(len(d.AG)):
            ag_recv(gs, s, q, True)
            if s < d.LONG:
                ag_send(gs, s, q, True)
            if s <= d.SHORT:
                ag_recv(gs, s, q, False)
                if s < d.SHORT:
                    ag_send(gs, s, q, False)
        to_partner(gs, s)
        if s <= d.SHORT:
            to_partner(gs, -s)

    def ag_partner(gs):
        for v in range(-d.SHORT, d.LONG + 1):
            recv(("ap", gs, v), hall.at[hrows(gs, 1 - k, ym(v))], partner)

    ag_start(0)
    send("dp", hall.at[mine_rows], hall.at[hrows(1, k, y)], {"dp": 1 - g})
    for s in range(1, d.LONG):
        ag_step(0, s)
    recv("dp", hall.at[hrows(1, k, y)], {"dp": 1 - g})
    ag_start(1)
    ag_step(0, d.LONG)
    ag_partner(0)

    def xrows(v):
        return rows(xm(v) * ZT, ZT)

    def x_first(t, m):
        a, b = t * F, (t + 1) * F
        xsend[t, 0] = po[xrows(2), a:b].astype(BF)
        send(("o0", t), xsend.at[t, 0], xrecv.at[t, 0], at_x(m))
        xsend[t, 1] = po[xrows(-m), a:b].astype(BF)
        send(("o1", t), xsend.at[t, 1], xrecv.at[t, 1], at_x(-m))

    def x_second(t, m):
        a, b = t * F, (t + 1) * F
        recv(("o0", t), xrecv.at[t, 0], at_x(m))
        xsend[t, 2] = (po[xrows(m), a:b] + xrecv[t, 0].astype(F32)).astype(BF)
        send(("o2", t), xsend.at[t, 2], xrecv.at[t, 2], at_x(m))

    def x_last(t, m):
        a, b = t * F, (t + 1) * F
        recv(("o1", t), xrecv.at[t, 1], at_x(-m))
        zs[:, a:b] = po[xrows(0), a:b] + xrecv[t, 1].astype(F32)
        recv(("o2", t), xrecv.at[t, 2], at_x(m))
        zs[:, a:b] += xrecv[t, 2].astype(F32)
        zsend[:, a:b] = zs[:, a:b].astype(BF)

    scale = 1.0 / math.sqrt(2 * R)
    WN = 2 * BLK

    def w_gu(gs, n):
        tk = slice(gs * R, gs * R + R)
        full = nn(xt[:, tk], hall[tk, HU + n : HU + n + WN])
        if gs == 0:
            acc_gu[:, n : n + WN] = full
            return
        full = ((full + acc_gu[:, n : n + WN]) * scale).astype(BF)
        for i in range(d.DB):
            for j in range(2):
                at = n // BLK + j
                dst, jj = (dg, at) if at < d.FB else (du, at - d.FB)
                dst[i * d.FB + jj] = full[i * BLK : (i + 1) * BLK, j * BLK : (j + 1) * BLK]

    def w_d(gs, n):
        tk = slice(gs * R, gs * R + R)
        full = nn(ht[:, tk], xr[1, tk, n : n + WN])
        if gs == 0:
            acc_d[:, n : n + WN] = full
            return
        full = ((full + acc_d[:, n : n + WN]) * scale).astype(BF)
        for i in range(d.FB):
            for j in range(2):
                dd[i * d.DB + n // BLK + j] = full[i * BLK : (i + 1) * BLK, j * BLK : (j + 1) * BLK]

    po[:, 0:F] = nn(hall[0:R, 0:HU], wd[...])
    x_first(0, 1)
    po[:, F : 2 * F] = nt(hall[0:R, HU:N], wgu[...])
    x_first(1, -1)
    ag_step(1, 1)
    steps = list(range(0, GU, WN))
    some = len(steps) // 2
    for n in steps[:some]:
        w_gu(0, n)
    x_second(0, 1)
    x_second(1, -1)
    ag_step(1, 2)
    for n in steps[some:]:
        w_gu(0, n)
    for s in range(3, d.LONG):
        ag_step(1, s)
    x_last(0, 1)
    x_last(1, -1)
    for o in range(1, d.Z):
        send(("oz", o), zsend.at[rows(zm(o) * T, T)], zrecv.at[o - 1], at_z(o))
    if d.LONG > 2:
        ag_step(1, d.LONG)
    ht[:, 0:R] = hall[0:R, 0:HU].T
    for n in range(0, F, WN):
        w_d(0, n)
    b_end(0)
    b_end(1)
    xt[:, R : 2 * R] = xr[0, R : 2 * R, :].T
    ag_partner(1)
    for buf in (dg, du, dd):
        buf[d.SL] = jnp.zeros((BLK, BLK), BF)

    def pick(ref, per, src, dst, out, sem):
        for s in range(d.CAP):
            at = ref[0, s] * per + ref[1, s]
            dst[s] = src[jnp.where(at < 0, jnp.int32(d.SL), at)]
        c = pltpu.make_async_copy(dst, out, sem)
        c.start()
        return c

    for n in steps:
        w_gu(1, n)
    outs = [pick(gi, d.FB, dg, pg, g_out, lsem.at[2]), pick(ui, d.FB, du, pu, u_out, lsem.at[3])]
    ht[:, R : 2 * R] = hall[R : 2 * R, 0:HU].T
    for n in range(0, F, WN):
        w_d(1, n)
    outs.append(pick(di, d.DB, dd, pd, d_out, lsem.at[4]))

    final = zs[rows(z * T, T), :]
    for o in range(1, d.Z):
        recv(("oz", o), zrecv.at[o - 1], at_z(o))
        final = final + zrecv[o - 1].astype(F32)
    fin[...] = final.astype(BF)
    outs.append(pltpu.make_async_copy(fin.at[:, 0:F], o_out, lsem.at[0]))
    outs.append(pltpu.make_async_copy(fin.at[:, F : 2 * F], ig_out, lsem.at[1]))
    outs[-1].start()
    outs[-2].start()
    for c in outs:
        c.wait()
    for c in sent:
        c.wait_send()


def pass_kernel(*refs):
    n = 5
    ins, outs, bufs, isem, osem = refs[:n], refs[n : 2 * n], refs[2 * n : 3 * n], refs[3 * n], refs[3 * n + 1]
    first = [pltpu.make_async_copy(ins[i], bufs[i], isem.at[i]) for i in range(n)]
    second = [pltpu.make_async_copy(bufs[i], outs[i], osem.at[i]) for i in range(n)]
    for c in first:
        c.start()
    for a, b in zip(first, second):
        a.wait()
        b.start()
    for c in second:
        c.wait()


def on_device(d, tokens, cotangent, gate_blocks, gate_index, up_blocks, up_index, down_blocks, down_index):
    T, F, HU, N, R = d.T, d.F, d.HU, d.N, d.R
    listings = [a[0, 0].T for a in (gate_index, up_index, down_index)]
    blocks = [a[0, 0] for a in (gate_blocks, up_blocks, down_blocks)]
    anyspace = pl.BlockSpec(memory_space=pl.ANY)
    smem = pl.BlockSpec(memory_space=pltpu.SMEM)
    V = pltpu.VMEM
    ZT = d.Z * T
    grads = jax.ShapeDtypeStruct((d.CAP, BLK, BLK), BF)
    act = jax.ShapeDtypeStruct((T, F), BF)
    shapes = [act, act, grads, grads, grads]
    results = pl.pallas_call(
        functools.partial(main_kernel, d),
        out_shape=shapes,
        in_specs=[smem] * 3 + [anyspace] * 5,
        out_specs=[anyspace] * 5,
        scratch_shapes=[
            pltpu.SMEM((3 * d.SL,), jnp.int32),
            *[V((d.CAP + 1, BLK, BLK), BF)] * 3,
            V((F, 2 * HU), BF),
            V((HU, F), BF),
            V((2, 2 * R, F), BF),
            V((2, R, F), BF),
            V((d.HALF, N), F32),
            V((d.HALF, N), F32),
            V((d.HALF, N), F32),
            V((d.LONG, T, N), BF),
            V((d.LONG, T, N), BF),
            V((d.SHORT, T, N), BF),
            V((d.SHORT, T, N), BF),
            V((T, N), F32),
            V((2 * R, N), BF),
            V((R, 2 * F), F32),
            V((2, 3, ZT, F), BF),
            V((2, 3, ZT, F), BF),
            V((ZT, 2 * F), F32),
            V((ZT, 2 * F), BF),
            V((d.Z - 1, T, 2 * F), BF),
            V((T, 2 * F), BF),
            V((F, 2 * R), BF),
            V((HU, 2 * R), BF),
            V((F, 2 * HU), F32),
            V((HU, F), F32),
            *[V((d.SL + 1, BLK, BLK), BF)] * 3,
            *[V((d.CAP, BLK, BLK), BF)] * 3,
            pltpu.SemaphoreType.DMA((5,)),
            pltpu.SemaphoreType.DMA((d.NSEM,)),
            pltpu.SemaphoreType.DMA((d.NSEM,)),
        ],
        compiler_params=pltpu.CompilerParams(
            collective_id=0, has_side_effects=True, vmem_limit_bytes=60 * 1024 * 1024
        ),
        name="ffn_main",
    )(*listings, tokens, cotangent, *blocks)
    o, ig, gg, ug, dgr = pl.pallas_call(
        pass_kernel,
        out_shape=shapes,
        in_specs=[anyspace] * 5,
        out_specs=[anyspace] * 5,
        scratch_shapes=[V(s.shape, BF) for s in shapes]
        + [pltpu.SemaphoreType.DMA((5,)), pltpu.SemaphoreType.DMA((5,))],
        compiler_params=pltpu.CompilerParams(vmem_limit_bytes=60 * 1024 * 1024),
        name="ffn_pass",
    )(*results)
    shape = gate_blocks.shape
    return (o, ig, gg.reshape(shape), ug.reshape(shape), dgr.reshape(shape))


def build(mesh, units):
    def body(tokens, cotangent, *rest):
        d = Dims(mesh.shape, tokens.shape[0], tokens.shape[1], rest[0].shape[2], units)
        return on_device(d, tokens, cotangent, *rest)

    act = P(("dp", "col"), "row")
    blocks = P("row", "col", None, None, None)
    index = P("row", "col", None, None)
    return jax.shard_map(
        body,
        mesh=mesh,
        in_specs=(act, act, blocks, index, blocks, index, blocks, index),
        out_specs=(act, act, blocks, blocks, blocks),
        check_vma=False,
    )


def solution(mesh):
    return build(mesh, 7)
```

time: 336 us -> 82.3 us (0.24)
  the two profiles are of different devices: /device:TPU:8 before, /device:TPU:1 now
where the time goes in v1:
time: 82.3 us; the launch traced here: 82 us
  Pallas kernels  81.4 us (99%)
    pallas_call x1, Pallas kernels, on_device(): pl.pallas_call(functools.partial(main_kernel, d), out_shape=shapes, in_sp...  78.9 us
    pallas_call x1, Pallas kernels, on_device(): pl.pallas_call(pass_kernel, out_shape=shapes, in_specs=[anyspace] * 5, ou...  2.52 us

profile of v1, /device:TPU:1, one launch (start us, length us, event | category | flops | bytes accessed | tf_op | source)
XLA Modules:
  0.0 82.0 jit_solution(8430636437922265649)
XLA Ops:
  0.6 78.9 %ffn_main.1 = (bf16[16,512]{1,0:T(8,128)(2,1)}, bf16[16,512]{1,0:T(8,128)(2,1)}, bf16[21,128,128]{2,1,0:T(8,128)(2,1)}, bf16[21,128,128]{2,1,0:T(8,128)(2,1)}, bf16[21,128,128]{2,1,0:T(8,128)(2,1)}) custom-call(s32[2,21]{1,0:T(2,128)} %bitcast.18, s32[2,21]{1,0:T(2,128)} %bitcast.19, s32[2,21]{1,0:T(2,128)} %bitcast.20, bf16[16,512]{1,0:T(8,128)(2,1)} %tok.1, ...), custom_call_target="tpu_custom_call" | custom-call | tf_op jit(solution)/shard_map/ffn_main/pallas_call | solution.py:491
  79.5 2.5 %ffn_pass.1 = (bf16[16,512]{1,0:T(8,128)(2,1)}, bf16[16,512]{1,0:T(8,128)(2,1)}, bf16[21,128,128]{2,1,0:T(8,128)(2,1)}, bf16[21,128,128]{2,1,0:T(8,128)(2,1)}, bf16[21,128,128]{2,1,0:T(8,128)(2,1)}) custom-call(bf16[16,512]{1,0:T(8,128)(2,1)} %get-tuple-element.15.refs_0_, bf16[16,512]{1,0:T(8,128)(2,1)} %get-tuple-element.16.refs_1_, ...), custom_call_target="tpu_custom_call" | custom-call | tf_op jit(solution)/shard_map/ffn_pass/pallas_call | solution.py:534

commit v2 on v1

--- a/solution.py
+++ b/solution.py
@@ -35,8 +35,7 @@
         self.X = XS
         self.Z = mesh_shape["col"] // XS
         self.Y = mesh_shape["row"] // 2
-        self.LONG = self.Y // 2
-        self.SHORT = self.Y // 2 - 1
+        assert self.Y == 8 and self.X == 4
         self.NCOL = mesh_shape["col"]
         self.NROW = mesh_shape["row"]
         self.R = self.NCOL * self.T
@@ -50,7 +49,7 @@
 def main_kernel(
     d, gi, ui, di, tok, cot, gb, ub, db,
     o_out, ig_out, g_out, u_out, d_out,
-    inv, wb0, wb1, wb2, wgu, wd, xr, xp, psend, precv, s1, rlong, slong, rshort, sshort, tot, hall,
+    inv, wb0, wb1, wb2, wgu, wd, xr, xp, psend, precv, s1, rsend, rrecv, tot, hall,
     po, xsend, xrecv, zs, zsend, zrecv, fin, xt, ht, acc_gu, acc_d, dg, du, dd, pg, pu, pd,
     lsem, ssem, rsem,
 ):
@@ -117,7 +116,7 @@
 
     barrier = pltpu.get_barrier_semaphore()
     peers = [at_z(o) for o in range(1, d.Z)] + [at_other_z(o) for o in range(d.Z)]
-    peers += [at_x(1), at_x(-1), at_y(1), at_y(-1), partner]
+    peers += [at_x(v) for v in range(1, d.X)] + [at_y(v) for v in (1, -1, 2, -2)] + [partner]
     for p in peers:
         pl.semaphore_signal(barrier, inc=1, device_id=p, device_id_type=MESH)
 
@@ -138,20 +137,12 @@
         return xr.at[t, rows((xm(v) * d.Z + zm(-o)) * T, T)]
 
     def x_chunk(t, o, src):
-        send(("xr", t, o), src, chunk(t, 0, o), at_x(1))
-        send(("xl", t, o), src, chunk(t, 0, o), at_x(-1))
-
-    def x_pass(t, o):
-        m = 1 if t == 0 else -1
-        side = "xr" if t == 0 else "xl"
-        recv((side, t, o), chunk(t, -m, o), at_x(m))
-        send(("xx", t, o), chunk(t, -m, o), chunk(t, -m, o), at_x(m))
+        for v in (2, 1, -1):
+            send(("xc", t, o, v), src, chunk(t, 0, o), at_x(v))
 
     def x_end(t, o):
-        m = 1 if t == 0 else -1
-        side = "xl" if t == 0 else "xr"
-        recv((side, t, o), chunk(t, m, o), at_x(-m))
-        recv(("xx", t, o), chunk(t, 2, o), at_x(m))
+        for v in (2, 1, -1):
+            recv(("xc", t, o, v), chunk(t, -v, o), at_x(v))
 
     for t, src in ((0, tok), (1, cot)):
         for o in range(1, d.Z):
@@ -206,25 +197,15 @@
         return xr.at[t, rows(R + xm(v) * ZT, ZT)]
 
     def b_send(t):
-        send(("br", t), xblock(t, 0), xblock(t, 0), at_x(1))
-        send(("bl", t), xblock(t, 0), xblock(t, 0), at_x(-1))
-
-    def b_pass(t):
-        m = 1 if t == 0 else -1
-        recv(("br" if t == 0 else "bl", t), xblock(t, -m), at_x(m))
-        send(("bb", t), xblock(t, -m), xblock(t, -m), at_x(m))
+        for v in (2, 1, -1):
+            send(("xb", t, v), xblock(t, 0), xblock(t, 0), at_x(v))
 
     def b_end(t):
-        m = 1 if t == 0 else -1
-        recv(("bl" if t == 0 else "br", t), xblock(t, m), at_x(-m))
-        recv(("bb", t), xblock(t, 2), at_x(m))
+        for v in (2, 1, -1):
+            recv(("xb", t, v), xblock(t, -v), at_x(v))
 
     dense(0, d.FB)
-    for o in range(d.Z):
-        x_pass(0, o)
     dense(1, d.FB)
-    for o in range(d.Z):
-        x_pass(1, o)
     dense(2, d.DB)
     loads[0].wait()
     loads[1].wait()
@@ -244,51 +225,42 @@
         xp[t, H : 2 * H] = xr[t, rows(k * H, H), :]
     for q, (a, b, _) in enumerate(d.RS):
         part = nn(xp[0], wgu[:, a:b]) if b <= GU else nt(xp[1], wd[a - GU : b - GU, :])
-        psend[:, a:b] = part[0:H]
+        psend[:, a:b] = part[0:H].astype(BF)
         send(("p", q), psend.at[:, a:b], precv.at[:, a:b], partner)
         s1[:, a:b] = part[H : 2 * H]
 
-    def rs_long(s, q):
-        a, b, m = d.RS[q]
-        mine = s1[rows(ym(m * (d.LONG - s)) * T, T), a:b]
-        if s > 0:
-            recv(("rl", s - 1, q), rlong.at[s - 1, :, a:b], at_y(m))
-            mine = mine + rlong[s - 1, :, a:b].astype(F32)
-        slong[s, :, a:b] = mine.astype(BF)
-        send(("rl", s, q), slong.at[s, :, a:b], rlong.at[s, :, a:b], at_y(m))
-
-    def rs_short(s, q):
-        a, b, m = d.RS[q]
-        mine = s1[rows(ym(-m * (d.SHORT - s)) * T, T), a:b]
-        if s > 0:
-            recv(("rs", s - 1, q), rshort.at[s - 1, :, a:b], at_y(-m))
-            mine = mine + rshort[s - 1, :, a:b].astype(F32)
-        sshort[s, :, a:b] = mine.astype(BF)
-        send(("rs", s, q), sshort.at[s, :, a:b], rshort.at[s, :, a:b], at_y(-m))
-
-    for s in range(d.LONG):
-        for q, (a, b, _) in enumerate(d.RS):
-            if s == 0:
-                recv(("p", q), precv.at[:, a:b], partner)
-                s1[:, a:b] += precv[:, a:b]
-            rs_long(s, q)
-            if s < d.SHORT:
-                rs_short(s, q)
-        if s == 0:
-            for t in (0, 1):
-                z_other(t)
-                b_send(t)
-            xt[:, 0:R] = xr[0, 0:R, :].T
-        if s == d.LONG - 1:
-            b_pass(0)
-            b_pass(1)
+    def rs_first(slot, q, m, far, hop):
+        a, b, _ = d.RS[q]
+        rsend[slot, :, a:b] = s1[rows(ym(m * far) * T, T), a:b].astype(BF)
+        send(("r", slot, q), rsend.at[slot, :, a:b], rrecv.at[slot, :, a:b], at_y(m * hop))
+
+    def rs_got(slot, q, m, hop):
+        a, b, _ = d.RS[q]
+        recv(("r", slot, q), rrecv.at[slot, :, a:b], at_y(m * hop))
+        return rrecv[slot, :, a:b].astype(F32)
+
     for q, (a, b, m) in enumerate(d.RS):
-        mine = s1[rows(y * T, T), a:b]
-        if d.SHORT > 0:
-            recv(("rs", d.SHORT - 1, q), rshort.at[d.SHORT - 1, :, a:b], at_y(-m))
-            mine = mine + rshort[d.SHORT - 1, :, a:b].astype(F32)
-        recv(("rl", d.LONG - 1, q), rlong.at[d.LONG - 1, :, a:b], at_y(m))
-        tot[:, a:b] = mine + rlong[d.LONG - 1, :, a:b].astype(F32)
+        recv(("p", q), precv.at[:, a:b], partner)
+        s1[:, a:b] += precv[:, a:b].astype(F32)
+        rs_first(0, q, m, 4, 2)
+        rs_first(1, q, m, 3, 1)
+        rs_first(4, q, -m, 3, 1)
+        rs_first(3, q, m, 1, 1)
+        rs_first(6, q, -m, 1, 1)
+    for q, (a, b, m) in enumerate(d.RS):
+        full = s1[rows(ym(2 * m) * T, T), a:b] + rs_got(0, q, m, 2) + rs_got(1, q, m, 1)
+        rsend[2, :, a:b] = full.astype(BF)
+        send(("r", 2, q), rsend.at[2, :, a:b], rrecv.at[2, :, a:b], at_y(2 * m))
+        full = s1[rows(ym(-2 * m) * T, T), a:b] + rs_got(4, q, -m, 1)
+        rsend[5, :, a:b] = full.astype(BF)
+        send(("r", 5, q), rsend.at[5, :, a:b], rrecv.at[5, :, a:b], at_y(-2 * m))
+    for t in (0, 1):
+        z_other(t)
+        b_send(t)
+    xt[:, 0:R] = xr[0, 0:R, :].T
+    for q, (a, b, m) in enumerate(d.RS):
+        full = s1[rows(y * T, T), a:b] + rs_got(3, q, m, 1) + rs_got(6, q, -m, 1)
+        tot[:, a:b] = full + rs_got(2, q, m, 2) + rs_got(5, q, -m, 2)
 
     gate, up, gh = tot[:, 0:HU], tot[:, HU:GU], tot[:, GU:N]
     sig = jax.nn.sigmoid(gate)
@@ -300,78 +272,93 @@
     def hrows(gs, kk, yy):
         return rows(gs * R + (kk * d.Y + yy) * T, T)
 
-    def ag_send(gs, s, q, long):
-        a, b, m = d.AG[q]
-        m = m if long else -m
-        ref = hall.at[hrows(gs, k, ym(-m * s)), a:b]
-        send(("al" if long else "as", gs, s, q), ref, ref, at_y(m))
-
-    def ag_recv(gs, s, q, long):
-        a, b, m = d.AG[q]
-        m = m if long else -m
-        ref = hall.at[hrows(gs, k, ym(-m * s)), a:b]
-        recv(("al" if long else "as", gs, s - 1, q), ref, at_y(m))
+    def ag_ref(gs, v, q):
+        a, b, _ = d.AG[q]
+        return hall.at[hrows(gs, k, ym(v)), a:b]
+
+    def ag_send(gs, q, m, src, dst):
+        ref = ag_ref(gs, -m * src, q)
+        send(("a", gs, q, m * dst), ref, ref, at_y(m * (dst - src)))
+
+    def ag_recv(gs, q, m, dst):
+        recv(("a", gs, q, m * dst), ag_ref(gs, -m * dst, q), at_y(m))
 
     def to_partner(gs, v):
         ref = hall.at[hrows(gs, k, ym(v))]
         send(("ap", gs, v), ref, ref, partner)
 
     def ag_start(gs):
+        for dst in (2, 1):
+            for q, (_, _, m) in enumerate(d.AG):
+                ag_send(gs, q, m, 0, dst)
+                ag_send(gs, q, -m, 0, dst)
+        to_partner(gs, 0)
+
+    def ag_step(gs):
+        for q, (_, _, m) in enumerate(d.AG):
+            ag_recv(gs, q, m, 2)
+            ag_send(gs, q, m, 2, 3)
+            ag_send(gs, q, m, 2, 4)
+            ag_recv(gs, q, -m, 2)
+            ag_send(gs, q, -m, 2, 3)
+        for v in (2, -2):
+            to_partner(gs, v)
         for q in range(len(d.AG)):
-            ag_send(gs, 0, q, True)
-            if d.SHORT > 0:
-                ag_send(gs, 0, q, False)
-        to_partner(gs, 0)
-
-    def ag_step(gs, s):
+            ag_recv(gs, q, 1, 1)
+            ag_recv(gs, q, -1, 1)
+        for v in (1, -1):
+            to_partner(gs, v)
+
+    def ag_last(gs):
         for q in range(len(d.AG)):
-            ag_recv(gs, s, q, True)
-            if s < d.LONG:
-                ag_send(gs, s, q, True)
-            if s <= d.SHORT:
-                ag_recv(gs, s, q, False)
-                if s < d.SHORT:
-                    ag_send(gs, s, q, False)
-        to_partner(gs, s)
-        if s <= d.SHORT:
-            to_partner(gs, -s)
+            ag_recv(gs, q, 1, 3)
+            ag_recv(gs, q, -1, 3)
+        for v in (3, -3):
+            to_partner(gs, v)
+        for q, (_, _, m) in enumerate(d.AG):
+            ag_recv(gs, q, m, 4)
+        to_partner(gs, 4)
 
     def ag_partner(gs):
-        for v in range(-d.SHORT, d.LONG + 1):
+        for v in range(-3, 5):
             recv(("ap", gs, v), hall.at[hrows(gs, 1 - k, ym(v))], partner)
 
     ag_start(0)
     send("dp", hall.at[mine_rows], hall.at[hrows(1, k, y)], {"dp": 1 - g})
-    for s in range(1, d.LONG):
-        ag_step(0, s)
+    ag_step(0)
+    ag_last(0)
     recv("dp", hall.at[hrows(1, k, y)], {"dp": 1 - g})
     ag_start(1)
-    ag_step(0, d.LONG)
-    ag_partner(0)
 
     def xrows(v):
         return rows(xm(v) * ZT, ZT)
 
-    def x_first(t, m):
+    FAR = (2, 1, -1)
+
+    def x_copy(t, i):
+        return pltpu.make_async_remote_copy(
+            src_ref=xsend.at[t, i], dst_ref=xrecv.at[t, i], send_sem=ssem.at[number(("ox", t, i))],
+            recv_sem=rsem.at[number(("ox", t, i))], device_id=at_x(FAR[i]), device_id_type=MESH,
+        )
+
+    def x_first(t, half):
+        for i, v in enumerate(FAR):
+
+            @pl.when(lax.div(xm(v), d.X // 2) == half)
+            def _(i=i, v=v):
+                xsend[t, i] = po[xrows(v), t * F : (t + 1) * F].astype(BF)
+                x_copy(t, i).start()
+
+    def x_last(t):
         a, b = t * F, (t + 1) * F
-        xsend[t, 0] = po[xrows(2), a:b].astype(BF)
-        send(("o0", t), xsend.at[t, 0], xrecv.at[t, 0], at_x(m))
-        xsend[t, 1] = po[xrows(-m), a:b].astype(BF)
-        send(("o1", t), xsend.at[t, 1], xrecv.at[t, 1], at_x(-m))
-
-    def x_second(t, m):
-        a, b = t * F, (t + 1) * F
-        recv(("o0", t), xrecv.at[t, 0], at_x(m))
-        xsend[t, 2] = (po[xrows(m), a:b] + xrecv[t, 0].astype(F32)).astype(BF)
-        send(("o2", t), xsend.at[t, 2], xrecv.at[t, 2], at_x(m))
-
-    def x_last(t, m):
-        a, b = t * F, (t + 1) * F
-        recv(("o1", t), xrecv.at[t, 1], at_x(-m))
-        zs[:, a:b] = po[xrows(0), a:b] + xrecv[t, 1].astype(F32)
-        recv(("o2", t), xrecv.at[t, 2], at_x(m))
-        zs[:, a:b] += xrecv[t, 2].astype(F32)
-        zsend[:, a:b] = zs[:, a:b].astype(BF)
+        full = po[xrows(0), a:b]
+        for i, v in enumerate(FAR):
+            recv(("ox", t, i), xrecv.at[t, i], at_x(v))
+            full = full + xrecv[t, i].astype(F32)
+        zs[:, a:b] = full
+        zsend[t] = full.astype(BF)
+        for o in range(1, d.Z):
+            send(("oz", t, o), zsend.at[t, rows(zm(o) * T, T)], zrecv.at[t, o - 1], at_z(o))
 
     scale = 1.0 / math.sqrt(2 * R)
     WN = 2 * BLK
@@ -400,31 +387,27 @@
             for j in range(2):
                 dd[i * d.DB + n // BLK + j] = full[i * BLK : (i + 1) * BLK, j * BLK : (j + 1) * BLK]
 
-    po[:, 0:F] = nn(hall[0:R, 0:HU], wd[...])
-    x_first(0, 1)
-    po[:, F : 2 * F] = nt(hall[0:R, HU:N], wgu[...])
-    x_first(1, -1)
-    ag_step(1, 1)
+    for half in (k, 1 - k):
+        rh = rows(half * H, H)
+        po[rh, 0:F] = nn(hall[rh, 0:HU], wd[...])
+        x_first(0, half)
+        po[rh, F : 2 * F] = nt(hall[rh, HU:N], wgu[...])
+        x_first(1, half)
+        if half is k:
+            ag_partner(0)
+    for t in (0, 1):
+        for i in range(len(FAR)):
+            sent.append(x_copy(t, i))
     steps = list(range(0, GU, WN))
-    some = len(steps) // 2
-    for n in steps[:some]:
+    for n in steps:
         w_gu(0, n)
-    x_second(0, 1)
-    x_second(1, -1)
-    ag_step(1, 2)
-    for n in steps[some:]:
-        w_gu(0, n)
-    for s in range(3, d.LONG):
-        ag_step(1, s)
-    x_last(0, 1)
-    x_last(1, -1)
-    for o in range(1, d.Z):
-        send(("oz", o), zsend.at[rows(zm(o) * T, T)], zrecv.at[o - 1], at_z(o))
-    if d.LONG > 2:
-        ag_step(1, d.LONG)
     ht[:, 0:R] = hall[0:R, 0:HU].T
     for n in range(0, F, WN):
         w_d(0, n)
+    ag_step(1)
+    x_last(0)
+    x_last(1)
+    ag_last(1)
     b_end(0)
     b_end(1)
     xt[:, R : 2 * R] = xr[0, R : 2 * R, :].T
@@ -448,11 +431,12 @@
         w_d(1, n)
     outs.append(pick(di, d.DB, dd, pd, d_out, lsem.at[4]))
 
-    final = zs[rows(z * T, T), :]
-    for o in range(1, d.Z):
-        recv(("oz", o), zrecv.at[o - 1], at_z(o))
-        final = final + zrecv[o - 1].astype(F32)
-    fin[...] = final.astype(BF)
+    for t in (0, 1):
+        full = zs[rows(z * T, T), t * F : (t + 1) * F]
+        for o in range(1, d.Z):
+            recv(("oz", t, o), zrecv.at[t, o - 1], at_z(o))
+            full = full + zrecv[t, o - 1].astype(F32)
+        fin[:, t * F : (t + 1) * F] = full.astype(BF)
     outs.append(pltpu.make_async_copy(fin.at[:, 0:F], o_out, lsem.at[0]))
     outs.append(pltpu.make_async_copy(fin.at[:, F : 2 * F], ig_out, lsem.at[1]))
     outs[-1].start()
@@ -500,21 +484,19 @@
             V((HU, F), BF),
             V((2, 2 * R, F), BF),
             V((2, R, F), BF),
+            V((d.HALF, N), BF),
+            V((d.HALF, N), BF),
             V((d.HALF, N), F32),
-            V((d.HALF, N), F32),
-            V((d.HALF, N), F32),
-            V((d.LONG, T, N), BF),
-            V((d.LONG, T, N), BF),
-            V((d.SHORT, T, N), BF),
-            V((d.SHORT, T, N), BF),
+            V((7, T, N), BF),
+            V((7, T, N), BF),
             V((T, N), F32),
             V((2 * R, N), BF),
             V((R, 2 * F), F32),
             V((2, 3, ZT, F), BF),
             V((2, 3, ZT, F), BF),
             V((ZT, 2 * F), F32),
-            V((ZT, 2 * F), BF),
-            V((d.Z - 1, T, 2 * F), BF),
+            V((2, ZT, F), BF),
+            V((2, d.Z - 1, T, F), BF),
             V((T, 2 * F), BF),
             V((F, 2 * R), BF),
             V((HU, 2 * R), BF),

time: 82.3 us -> 72.4 us (0.88)
  Pallas kernels: 81.4 us -> 71.5 us
    pallas_call x1, Pallas kernels: 78.9 us -> 69 us  [on_device(): pl.pallas_call(functools.partial(main_kernel, d), out_shape=shapes, in_sp...]
where the time goes in v2:
time: 72.4 us; the launch traced here: 72.2 us
  Pallas kernels  71.5 us (99%)
    pallas_call x1, Pallas kernels, on_device(): pl.pallas_call(functools.partial(main_kernel, d), out_shape=shapes, in_sp...  69 us
    pallas_call x1, Pallas kernels, on_device(): pl.pallas_call(pass_kernel, out_shape=shapes, in_specs=[anyspace] * 5, ou...  2.52 us

profile of v2, /device:TPU:1, one launch (start us, length us, event | category | flops | bytes accessed | tf_op | source)
XLA Modules:
  0.0 72.2 jit_solution(11887910628924889768)
XLA Ops:
  0.6 69.0 %ffn_main.1 = (bf16[16,512]{1,0:T(8,128)(2,1)}, bf16[16,512]{1,0:T(8,128)(2,1)}, bf16[21,128,128]{2,1,0:T(8,128)(2,1)}, bf16[21,128,128]{2,1,0:T(8,128)(2,1)}, bf16[21,128,128]{2,1,0:T(8,128)(2,1)}) custom-call(s32[2,21]{1,0:T(2,128)} %bitcast.18, s32[2,21]{1,0:T(2,128)} %bitcast.19, s32[2,21]{1,0:T(2,128)} %bitcast.20, bf16[16,512]{1,0:T(8,128)(2,1)} %tok.1, ...), custom_call_target="tpu_custom_call" | custom-call | tf_op jit(solution)/shard_map/ffn_main/pallas_call | solution.py:475
  69.6 2.5 %ffn_pass.1 = (bf16[16,512]{1,0:T(8,128)(2,1)}, bf16[16,512]{1,0:T(8,128)(2,1)}, bf16[21,128,128]{2,1,0:T(8,128)(2,1)}, bf16[21,128,128]{2,1,0:T(8,128)(2,1)}, bf16[21,128,128]{2,1,0:T(8,128)(2,1)}) custom-call(bf16[16,512]{1,0:T(8,128)(2,1)} %get-tuple-element.15.refs_0_, bf16[16,512]{1,0:T(8,128)(2,1)} %get-tuple-element.16.refs_1_, ...), custom_call_target="tpu_custom_call" | custom-call | tf_op jit(solution)/shard_map/ffn_pass/pallas_call | solution.py:516

commit v3 on v2

--- a/solution.py
+++ b/solution.py
@@ -42,7 +42,8 @@
         self.HALF = self.Y * self.T
         self.SL = self.DB * self.FB
         self.RS = split_tiles(3 * self.FB, 6, True)
-        self.AG = split_tiles(3 * self.FB, 4)
+        h, c = self.HU, (self.FB + 1) // 2 * BLK
+        self.AG = [[(0, c, -1), (c, h, 1)], [(h, 2 * h, -1), (2 * h, 3 * h, 1)]]
         self.NSEM = 256
 
 
@@ -209,21 +210,23 @@
     dense(2, d.DB)
     loads[0].wait()
     loads[1].wait()
-    for t in (0, 1):
+
+    def nt(a, b):
+        return lax.dot_general(a, b, (((1,), (1,)), ((), ())), preferred_element_type=F32)
+
+    def nn(a, b):
+        return jnp.dot(a, b, preferred_element_type=F32)
+
+    H = d.HALF
+
+    def halves(t):
         for o in range(d.Z):
             x_end(t, o)
-
-    def nt(a, b):
-        return lax.dot_general(a, b, (((1,), (1,)), ((), ())), preferred_element_type=F32)
-
-    def nn(a, b):
-        return jnp.dot(a, b, preferred_element_type=F32)
-
-    H = d.HALF
-    for t in (0, 1):
         xp[t, 0:H] = xr[t, rows((1 - k) * H, H), :]
         xp[t, H : 2 * H] = xr[t, rows(k * H, H), :]
-    for q, (a, b, _) in enumerate(d.RS):
+
+    def partial(q):
+        a, b, _ = d.RS[q]
         part = nn(xp[0], wgu[:, a:b]) if b <= GU else nt(xp[1], wd[a - GU : b - GU, :])
         psend[:, a:b] = part[0:H].astype(BF)
         send(("p", q), psend.at[:, a:b], precv.at[:, a:b], partner)
@@ -239,7 +242,8 @@
         recv(("r", slot, q), rrecv.at[slot, :, a:b], at_y(m * hop))
         return rrecv[slot, :, a:b].astype(F32)
 
-    for q, (a, b, m) in enumerate(d.RS):
+    def rs_start(q):
+        a, b, m = d.RS[q]
         recv(("p", q), precv.at[:, a:b], partner)
         s1[:, a:b] += precv[:, a:b].astype(F32)
         rs_first(0, q, m, 4, 2)
@@ -247,88 +251,109 @@
         rs_first(4, q, -m, 3, 1)
         rs_first(3, q, m, 1, 1)
         rs_first(6, q, -m, 1, 1)
-    for q, (a, b, m) in enumerate(d.RS):
+
+    def rs_second(q):
+        a, b, m = d.RS[q]
         full = s1[rows(ym(2 * m) * T, T), a:b] + rs_got(0, q, m, 2) + rs_got(1, q, m, 1)
         rsend[2, :, a:b] = full.astype(BF)
         send(("r", 2, q), rsend.at[2, :, a:b], rrecv.at[2, :, a:b], at_y(2 * m))
         full = s1[rows(ym(-2 * m) * T, T), a:b] + rs_got(4, q, -m, 1)
         rsend[5, :, a:b] = full.astype(BF)
         send(("r", 5, q), rsend.at[5, :, a:b], rrecv.at[5, :, a:b], at_y(-2 * m))
+
+    def rs_end(q):
+        a, b, m = d.RS[q]
+        full = s1[rows(y * T, T), a:b] + rs_got(3, q, m, 1) + rs_got(6, q, -m, 1)
+        tot[:, a:b] = full + rs_got(2, q, m, 2) + rs_got(5, q, -m, 2)
+
+    early = [q for q, (_, b, _) in enumerate(d.RS) if b <= GU]
+    late = [q for q, (_, b, _) in enumerate(d.RS) if b > GU]
+    for t, part in ((0, early), (1, late)):
+        halves(t)
+        for q in part:
+            partial(q)
+        for q in part:
+            rs_start(q)
+    for q in early + late:
+        rs_second(q)
     for t in (0, 1):
         z_other(t)
         b_send(t)
     xt[:, 0:R] = xr[0, 0:R, :].T
-    for q, (a, b, m) in enumerate(d.RS):
-        full = s1[rows(y * T, T), a:b] + rs_got(3, q, m, 1) + rs_got(6, q, -m, 1)
-        tot[:, a:b] = full + rs_got(2, q, m, 2) + rs_got(5, q, -m, 2)
-
+
+    def hrows(gs, kk, yy):
+        return rows(gs * R + (kk * d.Y + yy) * T, T)
+
+    def ag_ref(gs, v, c):
+        return hall.at[hrows(gs, k, ym(v)), c[0] : c[1]]
+
+    def ag_send(gs, c, m, src, dst):
+        ref = ag_ref(gs, -m * src, c)
+        send(("a", gs, c[0], m * dst), ref, ref, at_y(m * (dst - src)))
+
+    def ag_recv(gs, c, m, dst):
+        recv(("a", gs, c[0], m * dst), ag_ref(gs, -m * dst, c), at_y(m))
+
+    def to_partner(gs, grp, v):
+        ref = ag_ref(gs, v, (d.AG[grp][0][0], d.AG[grp][-1][1]))
+        send(("ap", gs, grp, v), ref, ref, partner)
+
+    def ag_start(gs, grp):
+        for dst in (2, 1):
+            for c in d.AG[grp]:
+                ag_send(gs, c, c[2], 0, dst)
+                ag_send(gs, c, -c[2], 0, dst)
+        to_partner(gs, grp, 0)
+
+    def ag_step(gs, grp):
+        for c in d.AG[grp]:
+            m = c[2]
+            ag_recv(gs, c, m, 2)
+            ag_send(gs, c, m, 2, 3)
+            ag_send(gs, c, m, 2, 4)
+            ag_recv(gs, c, -m, 2)
+            ag_send(gs, c, -m, 2, 3)
+        for v in (2, -2):
+            to_partner(gs, grp, v)
+        for c in d.AG[grp]:
+            ag_recv(gs, c, 1, 1)
+            ag_recv(gs, c, -1, 1)
+        for v in (1, -1):
+            to_partner(gs, grp, v)
+
+    def ag_last(gs, grp):
+        for c in d.AG[grp]:
+            ag_recv(gs, c, 1, 3)
+            ag_recv(gs, c, -1, 3)
+        for v in (3, -3):
+            to_partner(gs, grp, v)
+        for c in d.AG[grp]:
+            ag_recv(gs, c, c[2], 4)
+        to_partner(gs, grp, 4)
+
+    def ag_partner(gs, grp):
+        a, b = d.AG[grp][0][0], d.AG[grp][-1][1]
+        for v in range(-3, 5):
+            recv(("ap", gs, grp, v), hall.at[hrows(gs, 1 - k, ym(v)), a:b], partner)
+
+    mine_rows = rows((k * d.Y + y) * T, T)
+    for q in early:
+        rs_end(q)
+    gate, up = tot[:, 0:HU], tot[:, HU:GU]
+    sig = jax.nn.sigmoid(gate)
+    hall[mine_rows, 0:HU] = (gate * sig * up).astype(BF)
+    ag_start(0, 0)
+    for q in late:
+        rs_end(q)
     gate, up, gh = tot[:, 0:HU], tot[:, HU:GU], tot[:, GU:N]
     sig = jax.nn.sigmoid(gate)
-    mine_rows = rows((k * d.Y + y) * T, T)
-    hall[mine_rows, 0:HU] = (gate * sig * up).astype(BF)
     hall[mine_rows, HU:GU] = (gh * up * sig * (1.0 + gate * (1.0 - sig))).astype(BF)
     hall[mine_rows, GU:N] = (gh * gate * sig).astype(BF)
-
-    def hrows(gs, kk, yy):
-        return rows(gs * R + (kk * d.Y + yy) * T, T)
-
-    def ag_ref(gs, v, q):
-        a, b, _ = d.AG[q]
-        return hall.at[hrows(gs, k, ym(v)), a:b]
-
-    def ag_send(gs, q, m, src, dst):
-        ref = ag_ref(gs, -m * src, q)
-        send(("a", gs, q, m * dst), ref, ref, at_y(m * (dst - src)))
-
-    def ag_recv(gs, q, m, dst):
-        recv(("a", gs, q, m * dst), ag_ref(gs, -m * dst, q), at_y(m))
-
-    def to_partner(gs, v):
-        ref = hall.at[hrows(gs, k, ym(v))]
-        send(("ap", gs, v), ref, ref, partner)
-
-    def ag_start(gs):
-        for dst in (2, 1):
-            for q, (_, _, m) in enumerate(d.AG):
-                ag_send(gs, q, m, 0, dst)
-                ag_send(gs, q, -m, 0, dst)
-        to_partner(gs, 0)
-
-    def ag_step(gs):
-        for q, (_, _, m) in enumerate(d.AG):
-            ag_recv(gs, q, m, 2)
-            ag_send(gs, q, m, 2, 3)
-            ag_send(gs, q, m, 2, 4)
-            ag_recv(gs, q, -m, 2)
-            ag_send(gs, q, -m, 2, 3)
-        for v in (2, -2):
-            to_partner(gs, v)
-        for q in range(len(d.AG)):
-            ag_recv(gs, q, 1, 1)
-            ag_recv(gs, q, -1, 1)
-        for v in (1, -1):
-            to_partner(gs, v)
-
-    def ag_last(gs):
-        for q in range(len(d.AG)):
-            ag_recv(gs, q, 1, 3)
-            ag_recv(gs, q, -1, 3)
-        for v in (3, -3):
-            to_partner(gs, v)
-        for q, (_, _, m) in enumerate(d.AG):
-            ag_recv(gs, q, m, 4)
-        to_partner(gs, 4)
-
-    def ag_partner(gs):
-        for v in range(-3, 5):
-            recv(("ap", gs, v), hall.at[hrows(gs, 1 - k, ym(v))], partner)
-
-    ag_start(0)
+    ag_start(0, 1)
     send("dp", hall.at[mine_rows], hall.at[hrows(1, k, y)], {"dp": 1 - g})
-    ag_step(0)
-    ag_last(0)
-    recv("dp", hall.at[hrows(1, k, y)], {"dp": 1 - g})
-    ag_start(1)
+    ag_step(0, 0)
+    ag_step(0, 1)
+    ag_last(0, 0)
 
     def xrows(v):
         return rows(xm(v) * ZT, ZT)
@@ -387,14 +412,26 @@
             for j in range(2):
                 dd[i * d.DB + n // BLK + j] = full[i * BLK : (i + 1) * BLK, j * BLK : (j + 1) * BLK]
 
-    for half in (k, 1 - k):
+    def o_half(half):
         rh = rows(half * H, H)
         po[rh, 0:F] = nn(hall[rh, 0:HU], wd[...])
         x_first(0, half)
+
+    def ig_half(half):
+        rh = rows(half * H, H)
         po[rh, F : 2 * F] = nt(hall[rh, HU:N], wgu[...])
         x_first(1, half)
-        if half is k:
-            ag_partner(0)
+
+    o_half(k)
+    ag_partner(0, 0)
+    o_half(1 - k)
+    ag_last(0, 1)
+    ig_half(k)
+    recv("dp", hall.at[hrows(1, k, y)], {"dp": 1 - g})
+    ag_start(1, 0)
+    ag_start(1, 1)
+    ag_partner(0, 1)
+    ig_half(1 - k)
     for t in (0, 1):
         for i in range(len(FAR)):
             sent.append(x_copy(t, i))
@@ -404,14 +441,17 @@
     ht[:, 0:R] = hall[0:R, 0:HU].T
     for n in range(0, F, WN):
         w_d(0, n)
-    ag_step(1)
     x_last(0)
+    ag_step(1, 0)
+    ag_step(1, 1)
     x_last(1)
-    ag_last(1)
+    ag_last(1, 0)
+    ag_last(1, 1)
     b_end(0)
     b_end(1)
     xt[:, R : 2 * R] = xr[0, R : 2 * R, :].T
-    ag_partner(1)
+    ag_partner(1, 0)
+    ag_partner(1, 1)
     for buf in (dg, du, dd):
         buf[d.SL] = jnp.zeros((BLK, BLK), BF)
 

time: 72.4 us -> 73.6 us (1.017)
  Pallas kernels: 71.5 us -> 72.7 us
    pallas_call x1, Pallas kernels: 69 us -> 70.2 us  [on_device(): pl.pallas_call(functools.partial(main_kernel, d), out_shape=shapes, in_sp...]
where the time goes in v3:
time: 73.6 us; the launch traced here: 73.4 us
  Pallas kernels  72.7 us (99%)
    pallas_call x1, Pallas kernels, on_device(): pl.pallas_call(functools.partial(main_kernel, d), out_shape=shapes, in_sp...  70.2 us
    pallas_call x1, Pallas kernels, on_device(): pl.pallas_call(pass_kernel, out_shape=shapes, in_specs=[anyspace] * 5, ou...  2.52 us

profile of v3, /device:TPU:1, one launch (start us, length us, event | category | flops | bytes accessed | tf_op | source)
XLA Modules:
  0.0 73.4 jit_solution(5793458134083871188)
XLA Ops:
  0.6 70.2 %ffn_main.1 = (bf16[16,512]{1,0:T(8,128)(2,1)}, bf16[16,512]{1,0:T(8,128)(2,1)}, bf16[21,128,128]{2,1,0:T(8,128)(2,1)}, bf16[21,128,128]{2,1,0:T(8,128)(2,1)}, bf16[21,128,128]{2,1,0:T(8,128)(2,1)}) custom-call(s32[2,21]{1,0:T(2,128)} %bitcast.18, s32[2,21]{1,0:T(2,128)} %bitcast.19, s32[2,21]{1,0:T(2,128)} %bitcast.20, bf16[16,512]{1,0:T(8,128)(2,1)} %tok.1, ...), custom_call_target="tpu_custom_call" | custom-call | tf_op jit(solution)/shard_map/ffn_main/pallas_call | solution.py:515
  70.9 2.5 %ffn_pass.1 = (bf16[16,512]{1,0:T(8,128)(2,1)}, bf16[16,512]{1,0:T(8,128)(2,1)}, bf16[21,128,128]{2,1,0:T(8,128)(2,1)}, bf16[21,128,128]{2,1,0:T(8,128)(2,1)}, bf16[21,128,128]{2,1,0:T(8,128)(2,1)}) custom-call(bf16[16,512]{1,0:T(8,128)(2,1)} %get-tuple-element.15.refs_0_, bf16[16,512]{1,0:T(8,128)(2,1)} %get-tuple-element.16.refs_1_, ...), custom_call_target="tpu_custom_call" | custom-call | tf_op jit(solution)/shard_map/ffn_pass/pallas_call | solution.py:556

commit v4 on v3

--- a/solution.py
+++ b/solution.py
@@ -51,7 +51,7 @@
     d, gi, ui, di, tok, cot, gb, ub, db,
     o_out, ig_out, g_out, u_out, d_out,
     inv, wb0, wb1, wb2, wgu, wd, xr, xp, psend, precv, s1, rsend, rrecv, tot, hall,
-    po, xsend, xrecv, zs, zsend, zrecv, fin, xt, ht, acc_gu, acc_d, dg, du, dd, pg, pu, pd,
+    po, xsend, xrecv, zs, zsend, zrecv, xt, ht, acc_gu, acc_d, dg, du, dd,
     lsem, ssem, rsem,
 ):
     g = lax.axis_index("dp")
@@ -129,7 +129,7 @@
         pltpu.make_async_copy(ub, wb1.at[pl.ds(0, d.CAP)], lsem.at[3]),
         pltpu.make_async_copy(db, wb2.at[pl.ds(0, d.CAP)], lsem.at[4]),
     ]
-    for c in loads:
+    for c in loads[:2]:
         c.start()
 
     pl.semaphore_wait(barrier, len(peers))
@@ -149,6 +149,9 @@
         for o in range(1, d.Z):
             send(("z0", t, o), src, xr.at[t, own_rows], at_z(o))
         x_chunk(t, 0, src)
+
+    for c in loads[2:]:
+        c.start()
 
     for t, (ref, per) in enumerate(((gi, d.FB), (ui, d.FB), (di, d.DB))):
         wblk[t][d.CAP] = jnp.zeros((BLK, BLK), BF)
@@ -336,6 +339,19 @@
         for v in range(-3, 5):
             recv(("ap", gs, grp, v), hall.at[hrows(gs, 1 - k, ym(v)), a:b], partner)
 
+    def over_dp(grp):
+        cols = slice(0, HU) if grp == 0 else slice(HU, N)
+        i = number(("dp", grp))
+        return pltpu.make_async_remote_copy(
+            src_ref=hall.at[mine_rows, cols], dst_ref=hall.at[hrows(1, k, y), cols], send_sem=ssem.at[i],
+            recv_sem=rsem.at[i], device_id={"dp": 1 - g}, device_id_type=MESH,
+        )
+
+    def dp_landed(grp):
+        cols = slice(0, HU) if grp == 0 else slice(HU, N)
+        recv(("dp", grp), hall.at[hrows(1, k, y), cols], {"dp": 1 - g})
+        sent.append(over_dp(grp))
+
     mine_rows = rows((k * d.Y + y) * T, T)
     for q in early:
         rs_end(q)
@@ -343,6 +359,7 @@
     sig = jax.nn.sigmoid(gate)
     hall[mine_rows, 0:HU] = (gate * sig * up).astype(BF)
     ag_start(0, 0)
+    over_dp(0).start()
     for q in late:
         rs_end(q)
     gate, up, gh = tot[:, 0:HU], tot[:, HU:GU], tot[:, GU:N]
@@ -350,9 +367,11 @@
     hall[mine_rows, HU:GU] = (gh * up * sig * (1.0 + gate * (1.0 - sig))).astype(BF)
     hall[mine_rows, GU:N] = (gh * gate * sig).astype(BF)
     ag_start(0, 1)
-    send("dp", hall.at[mine_rows], hall.at[hrows(1, k, y)], {"dp": 1 - g})
+    over_dp(1).start()
     ag_step(0, 0)
     ag_step(0, 1)
+    dp_landed(0)
+    ag_start(1, 0)
     ag_last(0, 0)
 
     def xrows(v):
@@ -425,79 +444,65 @@
     o_half(k)
     ag_partner(0, 0)
     o_half(1 - k)
+    dp_landed(1)
+    ag_start(1, 1)
     ag_last(0, 1)
     ig_half(k)
-    recv("dp", hall.at[hrows(1, k, y)], {"dp": 1 - g})
-    ag_start(1, 0)
-    ag_start(1, 1)
     ag_partner(0, 1)
     ig_half(1 - k)
     for t in (0, 1):
         for i in range(len(FAR)):
             sent.append(x_copy(t, i))
     steps = list(range(0, GU, WN))
+    ag_step(1, 0)
     for n in steps:
         w_gu(0, n)
     ht[:, 0:R] = hall[0:R, 0:HU].T
     for n in range(0, F, WN):
         w_d(0, n)
     x_last(0)
-    ag_step(1, 0)
     ag_step(1, 1)
+    ag_last(1, 0)
     x_last(1)
-    ag_last(1, 0)
-    ag_last(1, 1)
     b_end(0)
     b_end(1)
     xt[:, R : 2 * R] = xr[0, R : 2 * R, :].T
     ag_partner(1, 0)
+    ht[:, R : 2 * R] = hall[R : 2 * R, 0:HU].T
+    for n in range(0, F, WN):
+        w_d(1, n)
+    ag_last(1, 1)
     ag_partner(1, 1)
     for buf in (dg, du, dd):
         buf[d.SL] = jnp.zeros((BLK, BLK), BF)
 
-    def pick(ref, per, src, dst, out, sem):
+    def pick(ref, per, src, dst):
         for s in range(d.CAP):
             at = ref[0, s] * per + ref[1, s]
             dst[s] = src[jnp.where(at < 0, jnp.int32(d.SL), at)]
-        c = pltpu.make_async_copy(dst, out, sem)
-        c.start()
-        return c
-
+
+    pick(di, d.DB, dd, d_out)
     for n in steps:
         w_gu(1, n)
-    outs = [pick(gi, d.FB, dg, pg, g_out, lsem.at[2]), pick(ui, d.FB, du, pu, u_out, lsem.at[3])]
-    ht[:, R : 2 * R] = hall[R : 2 * R, 0:HU].T
-    for n in range(0, F, WN):
-        w_d(1, n)
-    outs.append(pick(di, d.DB, dd, pd, d_out, lsem.at[4]))
-
-    for t in (0, 1):
+    pick(gi, d.FB, dg, g_out)
+    pick(ui, d.FB, du, u_out)
+
+    for t, out in ((0, o_out), (1, ig_out)):
         full = zs[rows(z * T, T), t * F : (t + 1) * F]
         for o in range(1, d.Z):
             recv(("oz", t, o), zrecv.at[t, o - 1], at_z(o))
             full = full + zrecv[t, o - 1].astype(F32)
-        fin[:, t * F : (t + 1) * F] = full.astype(BF)
-    outs.append(pltpu.make_async_copy(fin.at[:, 0:F], o_out, lsem.at[0]))
-    outs.append(pltpu.make_async_copy(fin.at[:, F : 2 * F], ig_out, lsem.at[1]))
-    outs[-1].start()
-    outs[-2].start()
-    for c in outs:
-        c.wait()
+        out[...] = full.astype(BF)
     for c in sent:
         c.wait_send()
 
 
 def pass_kernel(*refs):
     n = 5
-    ins, outs, bufs, isem, osem = refs[:n], refs[n : 2 * n], refs[2 * n : 3 * n], refs[3 * n], refs[3 * n + 1]
-    first = [pltpu.make_async_copy(ins[i], bufs[i], isem.at[i]) for i in range(n)]
-    second = [pltpu.make_async_copy(bufs[i], outs[i], osem.at[i]) for i in range(n)]
-    for c in first:
+    copies = [pltpu.make_async_copy(refs[i], refs[n + i], refs[2 * n].at[i]) for i in range(n)]
+    for c in copies:
         c.start()
-    for a, b in zip(first, second):
-        a.wait()
-        b.start()
-    for c in second:
+    for c in copies:
         c.wait()
 
 
@@ -514,9 +519,9 @@
     shapes = [act, act, grads, grads, grads]
     results = pl.pallas_call(
         functools.partial(main_kernel, d),
-        out_shape=shapes,
+        out_shape=[pltpu.VMEM(q.shape, q.dtype) for q in shapes],
         in_specs=[smem] * 3 + [anyspace] * 5,
-        out_specs=[anyspace] * 5,
+        out_specs=[pl.BlockSpec(memory_space=pltpu.VMEM)] * 5,
         scratch_shapes=[
             pltpu.SMEM((3 * d.SL,), jnp.int32),
             *[V((d.CAP + 1, BLK, BLK), BF)] * 3,
@@ -537,30 +542,27 @@
             V((ZT, 2 * F), F32),
             V((2, ZT, F), BF),
             V((2, d.Z - 1, T, F), BF),
-            V((T, 2 * F), BF),
             V((F, 2 * R), BF),
             V((HU, 2 * R), BF),
             V((F, 2 * HU), F32),
             V((HU, F), F32),
             *[V((d.SL + 1, BLK, BLK), BF)] * 3,
-            *[V((d.CAP, BLK, BLK), BF)] * 3,
             pltpu.SemaphoreType.DMA((5,)),
             pltpu.SemaphoreType.DMA((d.NSEM,)),
             pltpu.SemaphoreType.DMA((d.NSEM,)),
         ],
         compiler_params=pltpu.CompilerParams(
-            collective_id=0, has_side_effects=True, vmem_limit_bytes=60 * 1024 * 1024
+            collective_id=0, has_side_effects=True, vmem_limit_bytes=52 * 1024 * 1024
         ),
         name="ffn_main",
     )(*listings, tokens, cotangent, *blocks)
     o, ig, gg, ug, dgr = pl.pallas_call(
         pass_kernel,
         out_shape=shapes,
-        in_specs=[anyspace] * 5,
+        in_specs=[pl.BlockSpec(memory_space=pltpu.VMEM)] * 5,
         out_specs=[anyspace] * 5,
-        scratch_shapes=[V(s.shape, BF) for s in shapes]
-        + [pltpu.SemaphoreType.DMA((5,)), pltpu.SemaphoreType.DMA((5,))],
-        compiler_params=pltpu.CompilerParams(vmem_limit_bytes=60 * 1024 * 1024),
+        scratch_shapes=[pltpu.SemaphoreType.DMA((5,))],
+        compiler_params=pltpu.CompilerParams(vmem_limit_bytes=8 * 1024 * 1024),
         name="ffn_pass",
     )(*results)
     shape = gate_blocks.shape

time: 73.6 us -> 67.8 us (0.921)
  Pallas kernels: 72.7 us -> 67 us
    pallas_call x2, Pallas kernels: 72.7 us -> 67 us  [the longest x1 65.6 us: on_device(): pl.pallas_call(functools.partial(main_kernel, d), out_shape=[pltpu.VMEM(q...]
where the time goes in v4:
time: 67.8 us; the launch traced here: 67.7 us
  Pallas kernels  67 us (99%)
    pallas_call x1, Pallas kernels, on_device(): pl.pallas_call(functools.partial(main_kernel, d), out_shape=[pltpu.VMEM(q...  65.6 us
    pallas_call x1, Pallas kernels, on_device(): pl.pallas_call(pass_kernel, out_shape=shapes, in_specs=[pl.BlockSpec(memo...  1.36 us

profile of v4, /device:TPU:1, one launch (start us, length us, event | category | flops | bytes accessed | tf_op | source)
XLA Modules:
  0.0 67.7 jit_solution(9339137702635513836)
XLA Ops:
  0.6 65.6 %ffn_main.1 = (bf16[16,512]{1,0:T(8,128)(2,1)S(1)}, bf16[16,512]{1,0:T(8,128)(2,1)S(1)}, bf16[21,128,128]{2,1,0:T(8,128)(2,1)S(1)}, bf16[21,128,128]{2,1,0:T(8,128)(2,1)S(1)}, bf16[21,128,128]{2,1,0:T(8,128)(2,1)S(1)}) custom-call(s32[2,21]{1,0:T(2,128)} %bitcast.18, s32[2,21]{1,0:T(2,128)} %bitcast.19, s32[2,21]{1,0:T(2,128)} %bitcast.20, ...), custom_call_target="tpu_custom_call" | custom-call | tf_op jit(solution)/shard_map/ffn_main/pallas_call | solution.py:520
  66.3 1.4 %ffn_pass.1 = (bf16[16,512]{1,0:T(8,128)(2,1)}, bf16[16,512]{1,0:T(8,128)(2,1)}, bf16[21,128,128]{2,1,0:T(8,128)(2,1)}, bf16[21,128,128]{2,1,0:T(8,128)(2,1)}, bf16[21,128,128]{2,1,0:T(8,128)(2,1)}) custom-call(bf16[16,512]{1,0:T(8,128)(2,1)S(1)} %get-tuple-element.15.refs_0_, bf16[16,512]{1,0:T(8,128)(2,1)S(1)} %get-tuple-element.16.refs_1_, ...), custom_call_target="tpu_custom_call" | custom-call | tf_op jit(solution)/shard_map/ffn_pass/pallas_call | solution.py:559

commit v5 on v4

--- a/solution.py
+++ b/solution.py
@@ -455,15 +455,15 @@
             sent.append(x_copy(t, i))
     steps = list(range(0, GU, WN))
     ag_step(1, 0)
+    ag_step(1, 1)
     for n in steps:
         w_gu(0, n)
     ht[:, 0:R] = hall[0:R, 0:HU].T
     for n in range(0, F, WN):
         w_d(0, n)
     x_last(0)
-    ag_step(1, 1)
+    x_last(1)
     ag_last(1, 0)
-    x_last(1)
     b_end(0)
     b_end(1)
     xt[:, R : 2 * R] = xr[0, R : 2 * R, :].T

time: 67.8 us -> 67.5 us (level)
  no operation moved by 1% of the time
where the time goes in v5:
time: 67.5 us; the launch traced here: 67.4 us
  Pallas kernels  66.7 us (99%)
    pallas_call x1, Pallas kernels, on_device(): pl.pallas_call(functools.partial(main_kernel, d), out_shape=[pltpu.VMEM(q...  65.4 us
    pallas_call x1, Pallas kernels, on_device(): pl.pallas_call(pass_kernel, out_shape=shapes, in_specs=[pl.BlockSpec(memo...  1.36 us

profile of v5, /device:TPU:1, one launch (start us, length us, event | category | flops | bytes accessed | tf_op | source)
XLA Modules:
  0.0 67.4 jit_solution(5520771115853711403)
XLA Ops:
  0.6 65.4 %ffn_main.1 = (bf16[16,512]{1,0:T(8,128)(2,1)S(1)}, bf16[16,512]{1,0:T(8,128)(2,1)S(1)}, bf16[21,128,128]{2,1,0:T(8,128)(2,1)S(1)}, bf16[21,128,128]{2,1,0:T(8,128)(2,1)S(1)}, bf16[21,128,128]{2,1,0:T(8,128)(2,1)S(1)}) custom-call(s32[2,21]{1,0:T(2,128)} %bitcast.18, s32[2,21]{1,0:T(2,128)} %bitcast.19, s32[2,21]{1,0:T(2,128)} %bitcast.20, ...), custom_call_target="tpu_custom_call" | custom-call | tf_op jit(solution)/shard_map/ffn_main/pallas_call | solution.py:520
  66.0 1.4 %ffn_pass.1 = (bf16[16,512]{1,0:T(8,128)(2,1)}, bf16[16,512]{1,0:T(8,128)(2,1)}, bf16[21,128,128]{2,1,0:T(8,128)(2,1)}, bf16[21,128,128]{2,1,0:T(8,128)(2,1)}, bf16[21,128,128]{2,1,0:T(8,128)(2,1)}) custom-call(bf16[16,512]{1,0:T(8,128)(2,1)S(1)} %get-tuple-element.15.refs_0_, bf16[16,512]{1,0:T(8,128)(2,1)S(1)} %get-tuple-element.16.refs_1_, ...), custom_call_target="tpu_custom_call" | custom-call | tf_op jit(solution)/shard_map/ffn_pass/pallas_call | solution.py:559
